TPU v7x, 32 devices: a whole 2x2x4 slice. The times are simulated.
32 devices in a mesh: dp: 16 (over z, x, core), tensor: 2 (over y).
Axes of the slice: x: 2, y: 2, z: 4, core: 2. Of those that a mesh axis runs over, the one named last changes fastest.
Arguments:
- hidden_in: bfloat16 [20480, 768], P('dp'), may hold values from -6 to 6
- cotangent: bfloat16 [20480, 768], P('dp'), may hold values from -6 to 6
- prompt_start: int32 [4], replicated, may hold values from 0 to 511
- cont_gap: int32 [4, 12], replicated, may hold values from 0 to 511
- seg_len: int32 [6, 3], replicated, may hold values from 256 to 5120, as said below
- dilation_rate: int32 [6, 3], replicated, may hold values from 1 to 6, as said below
- pre_gain: bfloat16 [768], replicated, may hold values from 0.5 to 1.5
- pre_bias: bfloat16 [768], replicated, may hold values from -1 to 1
- query_weight: bfloat16 [768, 768], P(None, 'tensor'), may hold values from -0.21875 to 0.21875
- query_bias: bfloat16 [768], P('tensor'), may hold values from -1 to 1
- key_weight: bfloat16 [768, 768], P(None, 'tensor'), may hold values from -0.21875 to 0.21875
- value_weight: bfloat16 [768, 768], P(None, 'tensor'), may hold values from -0.21875 to 0.21875
- value_bias: bfloat16 [768], P('tensor'), may hold values from -1 to 1
- sub_gain: bfloat16 [768], P('tensor'), may hold values from 0.5 to 1.5
- sub_bias: bfloat16 [768], P('tensor'), may hold values from -1 to 1
- out_weight: bfloat16 [768, 768], P('tensor'), may hold values from -0.21875 to 0.21875
- out_bias: bfloat16 [768], replicated, may hold values from -1 to 1
- mid_gain: bfloat16 [768], replicated, may hold values from 0.5 to 1.5
- mid_bias: bfloat16 [768], replicated, may hold values from -1 to 1
- inner_weight: bfloat16 [768, 3072], P(None, 'tensor'), may hold values from -0.21875 to 0.21875
- inner_bias: bfloat16 [3072], P('tensor'), may hold values from -1 to 1
- ffn_gain: bfloat16 [3072], P('tensor'), may hold values from 0.5 to 1.5
- ffn_bias: bfloat16 [3072], P('tensor'), may hold values from -1 to 1
- outer_weight: bfloat16 [3072, 768], P('tensor'), may hold values from -0.109375 to 0.109375
- outer_bias: bfloat16 [768], replicated, may hold values from -1 to 1
Outputs:
- output: bfloat16 [20480, 768], P('dp')
- input_grad: bfloat16 [20480, 768], P('dp')
- pre_gain_grad: float32 [768], P('dp')
- pre_bias_grad: float32 [768], P('dp')
- query_weight_grad: float32 [768, 768], P('dp', 'tensor')
- query_bias_grad: float32 [768], P(('tensor', 'dp'))
- key_weight_grad: float32 [768, 768], P('dp', 'tensor')
- value_weight_grad: float32 [768, 768], P('dp', 'tensor')
- value_bias_grad: float32 [768], P(('tensor', 'dp'))
- sub_gain_grad: float32 [768], P(('tensor', 'dp'))
- sub_bias_grad: float32 [768], P(('tensor', 'dp'))
- out_weight_grad: float32 [768, 768], P('tensor', 'dp')
- out_bias_grad: float32 [768], P('dp')
- mid_gain_grad: float32 [768], P('dp')
- mid_bias_grad: float32 [768], P('dp')
- inner_weight_grad: float32 [768, 3072], P('dp', 'tensor')
- inner_bias_grad: float32 [3072], P(('tensor', 'dp'))
- ffn_gain_grad: float32 [3072], P(('tensor', 'dp'))
- ffn_bias_grad: float32 [3072], P(('tensor', 'dp'))
- outer_weight_grad: float32 [3072, 768], P('tensor', 'dp')
- outer_bias_grad: float32 [768], P('dp')
Inputs may be any that keep to these rules, and one draw needn't show every extreme that they name: seg_len[a, c] is the segment length of configuration c of head pair a (heads 2a and 2a + 1); one segment of the last configuration holds every position of a group. dilation_rate[a, 0] = 1 for every head pair a.
All inputs are finite; a program needn't handle non-finite values.
Results may differ from a plain program's by a relative error of at most 0.017.
Values may be sent and summed in bfloat16 or wider, within the bound.
A program may use at most 256 MiB of HBM per device.

v0:
```python
import functools

import jax
import jax.numpy as jnp
from jax import lax
from jax.experimental import pallas as pl
from jax.experimental.pallas import tpu as pltpu
from jax.sharding import PartitionSpec as P

HD = 64
PROMPT = 2048
CONT = 256
GDEV = 4
TILE = 256
CHUNK = PROMPT // GDEV
PTILES = CHUNK // TILE
LOG2E = 1.4426950408889634
BF = jnp.bfloat16
F32 = jnp.float32
D = 768
EPSILON = 1e-05
MESH = pl.DeviceIdType.MESH


def dot_nt(a, b):
    return lax.dot_general(a, b, (((1,), (1,)), ((), ())), preferred_element_type=F32)


def dot_nn(a, b):
    return lax.dot_general(a, b, (((1,), (0,)), ((), ())), preferred_element_type=F32)


def low_half(rows):
    return lax.broadcasted_iota(jnp.int32, (rows, 128), 1) < HD


def settings(seg, rate, pair):
    def row(value):
        return jnp.broadcast_to(value, (1, 128)).astype(F32)

    def rest(number, period):
        return number - period * jnp.floor((number + 0.5) / period)

    at = pl.ds(pair, 1)
    second, third = row(rate[at, 1:2]), row(rate[at, 2:3])
    head = jnp.full((1, 128), 2 * pair, jnp.int32).astype(F32)
    return (
        1.0 / row(seg[at, 0:1]),
        1.0 / row(seg[at, 1:2]),
        second,
        1.0 / second,
        third,
        1.0 / third,
        rest(head, second),
        rest(head + 1.0, second),
        rest(head, third),
        rest(head + 1.0, third),
    )


def codes(at, cells, miss):
    first = jnp.floor((at + 0.5) * cells[0])
    second = jnp.floor((at + 0.5) * cells[1])
    rest1 = at - cells[2] * jnp.floor((at + 0.5) * cells[3])
    rest2 = at - cells[4] * jnp.floor((at + 0.5) * cells[5])
    return [
        first,
        jnp.where(rest1 == cells[6], second, miss),
        jnp.where(rest1 == cells[7], second, miss),
        jnp.where(rest2 == cells[8], 1.0, 0.0),
        jnp.where(rest2 == cells[9], 1.0, 0.0),
    ]


def bit_peer(device, bit):
    step = 1 << bit
    return device + (1 - 2 * ((device // step) % 2)) * step


def greet(peers):
    barrier = pltpu.get_barrier_semaphore()
    for peer in peers:
        pl.semaphore_signal(barrier, inc=1, device_id=peer, device_id_type=MESH)
    pl.semaphore_wait(barrier, len(peers))


def xor_bits(a, b):
    return (a % 2 + b % 2) % 2 + 2 * ((a // 2 + b // 2) % 2)


def fwd_kernel(
    starts, gaps, seg, rate, hid, vec, wq, wk, wv, w1, wo, vec_hbm,
    e_ref, li_ref, q_out, k_out, v_out, kp_out, vp_out, o_out, mine_out, got_out,
    w1_got, w1_swap, wo_got, wo_swap, vec_got,
    t_s, kc_s, kv_s, low_s, q_s, ko_s, vo_s, o_s, sems_a, sems_b, loc_sems,
):
    pair = pl.program_id(0)
    step = pl.program_id(1)
    pairs = pl.num_programs(0)
    device = lax.axis_index("dp")
    side = lax.axis_index("tensor")
    member = device % GDEV
    core = device % 2
    rows, width = q_s.shape
    n_pairs = width // 128
    last_pair = n_pairs - 1
    conts = rows - CHUNK
    near = {"dp": bit_peer(device, 0), "tensor": side}
    far = {"dp": bit_peer(device, 1), "tensor": side}
    across = {"dp": device, "tensor": 1 - side}
    half_u = w1.shape[1] // 2
    half_w = wo.shape[0] // 2
    half_p, half_c = CHUNK // 2, conts // 2
    sent_u = pl.multiple_of(core * half_u, 128)
    shared_at = 2 * D + 2 * width
    sent_w = pl.multiple_of(core * half_w, 64)

    def remote(i, src, dst, peer):
        return pltpu.make_async_remote_copy(
            src_ref=src, dst_ref=dst, send_sem=sems_a.at[i], recv_sem=sems_b.at[i], device_id=peer, device_id_type=MESH
        )

    def to_far(p):
        lanes = pl.ds(p * 128, 128)
        return remote(3 * p, kv_s.at[0, :, :, lanes], kv_s.at[2, :, :, lanes], far)

    def to_near(p):
        lanes = pl.ds(p * 128, 128)
        return remote(3 * p + 1, kv_s.at[0, :, :, lanes], kv_s.at[1, :, :, lanes], near)

    def relay(p):
        lanes = pl.ds(p * 128, 128)
        return remote(3 * p + 2, kv_s.at[2, :, :, lanes], kv_s.at[3, :, :, lanes], near)

    base = 3 * n_pairs
    fetch_y = [
        remote(base, wo.at[pl.ds(sent_w, half_w), :], wo_got, across),
        remote(base + 1, w1.at[:, pl.ds(sent_u, half_u)], w1_got, across),
        remote(base + 2, vec_hbm.at[:, pl.ds(shared_at, vec_got.shape[1])], vec_got, across),
    ]
    fetch_core = [
        remote(base + 3, wo_got, wo_swap, near),
        remote(base + 4, w1_got, w1_swap, near),
    ]

    def give(p, piece):
        lanes = pl.ds(p * 128, 128)
        their_p = pl.multiple_of((1 - side) * half_p, 128)
        their_c = pl.multiple_of(CHUNK + (1 - side) * half_c, 128)
        third = half_c // 3
        if piece == 0:
            source, target = pl.ds(their_p, half_p), pl.ds(0, half_p)
        else:
            source = pl.ds(pl.multiple_of(their_c + (piece - 1) * third, 128), third)
            target = pl.ds(half_p + (piece - 1) * third, third)
        return remote(base + 5 + 4 * p + piece, o_s.at[source, lanes], got_out.at[target, lanes], across)

    def keeps():
        own_p = pl.multiple_of(side * half_p, 128)
        own_c = pl.multiple_of(CHUNK + side * half_c, 128)
        return [
            pltpu.make_async_copy(o_s, o_out, loc_sems.at[0]),
            pltpu.make_async_copy(o_s.at[pl.ds(own_p, half_p), :], mine_out.at[pl.ds(0, half_p), :], loc_sems.at[1]),
            pltpu.make_async_copy(o_s.at[pl.ds(own_c, half_c), :], mine_out.at[pl.ds(half_p, half_c), :], loc_sems.at[2]),
        ]

    def saves():
        out = [
            pltpu.make_async_copy(q_s, q_out, loc_sems.at[3]),
            pltpu.make_async_copy(ko_s, k_out, loc_sems.at[0]),
            pltpu.make_async_copy(vo_s, v_out, loc_sems.at[5]),
        ]
        for r in range(GDEV):
            span = pl.ds(r * CHUNK, CHUNK)
            out.append(pltpu.make_async_copy(kv_s.at[r, 0], kp_out.at[span, :], loc_sems.at[6 + 2 * r]))
            out.append(pltpu.make_async_copy(kv_s.at[r, 1], vp_out.at[span, :], loc_sems.at[7 + 2 * r]))
        return out

    @pl.when((pair == 0) & (step == 0))
    def _():
        greet([near, far, across])
        for copy in fetch_y:
            copy.start()
        gain_f, bias_f = vec[:, pl.ds(0, D)], vec[:, pl.ds(D, D)]
        query_bias = vec[:, pl.ds(2 * D, width)]
        value_bias = vec[:, pl.ds(2 * D + width, width)]

        def norm(at, size):
            x = hid[at : at + size, :].astype(F32)
            center = jnp.mean(x, axis=1, keepdims=True)
            scale = lax.rsqrt(jnp.mean(x * x, axis=1, keepdims=True) - center * center + EPSILON)
            low = ((x - center) * scale * gain_f + bias_f).astype(BF)
            low_s[at : at + size, :] = low
            return low

        low = norm(0, CHUNK)
        kv_s[0, 0] = dot_nn(low, wk[...]).astype(BF)
        kv_s[0, 1] = (dot_nn(low, wv[...]) + value_bias).astype(BF)
        to_far(0).start()
        for p in range(n_pairs):
            to_near(p).start()
        for at in range(CHUNK, rows, TILE):
            low = norm(at, TILE)
            ko_s[at - CHUNK : at - CHUNK + TILE, :] = dot_nn(low, wk[...]).astype(BF)
            vo_s[at - CHUNK : at - CHUNK + TILE, :] = (dot_nn(low, wv[...]) + value_bias).astype(BF)
        to_far(0).wait_send()
        for p in range(1, n_pairs):
            to_far(p).start()
        for at in range(0, rows, TILE):
            q_s[at : at + TILE, :] = ((dot_nn(low_s[at : at + TILE, :], wq[...]) + query_bias) * 0.125).astype(BF)
        to_far(0).wait_recv()
        relay(0).start()

    for p in range(n_pairs):
        @pl.when((pair == p) & (step == 0))
        def _():
            to_near(p).wait_recv()
            relay(p).wait_recv()

        if p + 1 < n_pairs:
            @pl.when((pair == p) & (step == 3))
            def _():
                to_far(p + 1).wait_recv()
                relay(p + 1).start()

    lanes = pl.ds(pl.multiple_of(pair * 128, 128), 128)
    low = low_half(TILE)
    q = q_s[pl.ds(pl.multiple_of(step * TILE, TILE), TILE), lanes]
    zero = jnp.zeros_like(q)
    qs = [jnp.where(low, q, zero), jnp.where(low, zero, q)]
    row = lax.broadcasted_iota(jnp.int32, (TILE, 128), 0).astype(F32)
    group = device // GDEV
    start = starts[group]
    first_cont = member * (conts // CONT)
    own_gap = gaps[group, first_cont + jnp.maximum(step - PTILES, 0)]
    base_q = start + jnp.where(step < PTILES, member * CHUNK + step * TILE, PROMPT + own_gap)
    cells = settings(seg, rate, side * n_pairs + pair)
    at_q = base_q.astype(F32) + row
    qc = codes(at_q, cells, -2.0)

    @pl.when(step == 0)
    def _():
        ahead = lax.broadcasted_iota(jnp.int32, (8, 128), 1).astype(F32) + start.astype(F32)
        for j in range(PROMPT // 128):
            for i, c in enumerate(codes(ahead + j * 128.0, cells, -1.0)):
                kc_s[i, :, j * 128 : (j + 1) * 128] = c

    def logits(mx, keys, kc, causal, at, span):
        out = []
        for h in range(2):
            s = dot_nt(qs[h], keys)
            top = mx[h]
            for g in range(span // 128):
                part = slice(g * 128, (g + 1) * 128)
                w = jnp.where(qc[0] == kc[0][:, part], 1.0, 0.0)
                w = w + jnp.where(qc[1 + h] == kc[1 + h][:, part], 1.0, 0.0)
                w = w + qc[3 + h] * kc[3 + h][:, part]
                if causal is not None:
                    w = jnp.where(causal[:, part], w, 0.0)
                t = s[:, part] * LOG2E + jnp.log2(w)
                t_s[h, :, pl.ds(at + g * 128, 128)] = t
                top = jnp.maximum(top, t)
            out.append(top)
        return tuple(out)

    def weigh(carry, vals, m, at, span):
        sums, accs = carry
        ns, na = [], []
        for h in range(2):
            total = sums[h]
            parts = []
            for g in range(span // 128):
                e = jnp.exp2(t_s[h, :, pl.ds(at + g * 128, 128)] - m[h])
                total = total + e
                parts.append(e.astype(BF))
            el = jnp.concatenate(parts, axis=1)
            e_ref[h, :, pl.ds(at, span)] = el
            ns.append(total)
            na.append(accs[h] + dot_nn(el, vals))
        return (tuple(ns), tuple(na))

    def finish_rows(carry):
        sums, accs = carry
        li = [1.0 / jnp.sum(s, axis=1, keepdims=True) for s in sums]
        lfull = jnp.where(low, li[0], li[1])
        li_ref[...] = lfull
        o_s[pl.ds(pl.multiple_of(step * TILE, TILE), TILE), lanes] = (jnp.where(low, accs[0], accs[1]) * lfull).astype(BF)

    def tops(mx):
        return [jnp.broadcast_to(jnp.max(x, axis=1, keepdims=True), (TILE, 128)) for x in mx]

    neg = jnp.full((TILE, 128), -jnp.inf, F32)
    zf = jnp.zeros((TILE, 128), F32)

    def key_codes(at, span):
        return [kc_s[i, 0:1, pl.ds(at, span)] for i in range(5)]

    @pl.when(step < PTILES)
    def _():
        def one(j, mx):
            at = pl.multiple_of(j * CHUNK, CHUNK)
            held = xor_bits(j, member)
            return logits(
                mx, kv_s[held, 0, :, lanes], key_codes(at, CHUNK), None, pl.multiple_of(held * CHUNK, CHUNK), CHUNK
            )

        mx = lax.fori_loop(0, member, one, (neg, neg))
        at = pl.multiple_of(member * CHUNK, CHUNK)
        rows_id = lax.broadcasted_iota(jnp.int32, (TILE, CHUNK), 0) + step * TILE
        cols = lax.broadcasted_iota(jnp.int32, (TILE, CHUNK), 1)
        mx = logits(mx, kv_s[0, 0, :, lanes], key_codes(at, CHUNK), cols <= rows_id, 0, CHUNK)
        m = tops(mx)

        def two(j, carry):
            held = xor_bits(j, member)
            return weigh(carry, kv_s[held, 1, :, lanes], m, pl.multiple_of(held * CHUNK, CHUNK), CHUNK)

        finish_rows(lax.fori_loop(0, member + 1, two, ((zf, zf), (zf, zf))))

    @pl.when(step >= PTILES)
    def _():
        own = pl.ds(pl.multiple_of((step - PTILES) * TILE, TILE), TILE)
        mx = (neg, neg)
        for j in range(GDEV):
            at = pl.multiple_of(xor_bits(j, member) * CHUNK, CHUNK)
            mx = logits(mx, kv_s[j, 0, :, lanes], key_codes(at, CHUNK), None, j * CHUNK, CHUNK)
        rows_id = lax.broadcasted_iota(jnp.int32, (TILE, CONT), 0)
        cols = lax.broadcasted_iota(jnp.int32, (TILE, CONT), 1)
        ahead = lax.broadcasted_iota(jnp.int32, (8, 128), 1).astype(F32) + base_q.astype(F32)
        parts = [codes(ahead + j * 128.0, cells, -1.0) for j in range(CONT // 128)]
        own_codes = [jnp.concatenate([part[i] for part in parts], axis=1)[0:1] for i in range(5)]
        mx = logits(mx, ko_s[own, lanes], own_codes, cols <= rows_id, PROMPT, CONT)
        m = tops(mx)
        carry = ((zf, zf), (zf, zf))
        for j in range(GDEV):
            carry = weigh(carry, kv_s[j, 1, :, lanes], m, j * CHUNK, CHUNK)
        finish_rows(weigh(carry, vo_s[own, lanes], m, PROMPT, CONT))

    end = pl.num_programs(1) - 1
    for p in range(n_pairs):
        @pl.when((pair == p) & (step == 1 - side))
        def _():
            give(p, 0).start()

        for unit in range(6):
            @pl.when((pair == p) & (step == PTILES + unit // 2) & (side == 1 - unit // 3))
            def _():
                give(p, 1 + unit % 3).start()

    @pl.when((pair == last_pair - 1) & (step == 3))
    def _():
        for i in range(2):
            fetch_y[i].wait_recv()
            fetch_core[i].start()

    @pl.when((pair == last_pair) & (step == 0))
    def _():
        for copy in saves():
            copy.start()

    @pl.when((pair == last_pair) & (step == end))
    def _():
        for copy in keeps():
            copy.start()
        fetch_y[2].wait_recv()
        for copy in fetch_core:
            copy.wait_recv()
        for p in range(n_pairs):
            for piece in range(4):
                copy = give(p, piece)
                copy.wait_recv()
                copy.wait_send()
            if p > 0:
                to_far(p).wait_send()
            to_near(p).wait_send()
            relay(p).wait_send()
        for copy in fetch_y + fetch_core:
            copy.wait_send()
        for copy in keeps() + saves():
            copy.wait()


def attend(starts, gaps, seg, rate, hid, vec, wq, wk, wv, w1, wo):
    rows = hid.shape[0]
    width = wq.shape[1]
    pairs = width // 128
    span = PROMPT + CONT
    conts = rows - CHUNK
    units = w1.shape[1]
    vmem = pl.BlockSpec(memory_space=pltpu.VMEM)
    hbm = pl.BlockSpec(memory_space=pl.ANY)
    shape = jax.ShapeDtypeStruct
    copies = 3 * pairs + 5 + 4 * pairs
    shared = 3 * units + 2 * width
    smem = pl.BlockSpec(memory_space=pltpu.SMEM)
    return pl.pallas_call(
        fwd_kernel,
        grid_spec=pltpu.PrefetchScalarGridSpec(
            num_scalar_prefetch=0,
            grid=(pairs, rows // TILE),
            in_specs=[smem] * 2 + [vmem] * 7 + [hbm] * 3,
            out_specs=[
                pl.BlockSpec((2, TILE, span), lambda a, t: (a, t, 0)),
                pl.BlockSpec((TILE, 128), lambda a, t: (t, a)),
            ]
            + [hbm] * 13,
            scratch_shapes=[
                pltpu.VMEM((2, TILE, span), F32),
                pltpu.VMEM((5, 8, PROMPT), F32),
                pltpu.VMEM((GDEV, 2, CHUNK, width), BF),
                pltpu.VMEM((rows, D), BF),
                pltpu.VMEM((rows, width), BF),
                pltpu.VMEM((conts, width), BF),
                pltpu.VMEM((conts, width), BF),
                pltpu.VMEM((rows, width), BF),
                pltpu.SemaphoreType.DMA((copies,)),
                pltpu.SemaphoreType.DMA((copies,)),
                pltpu.SemaphoreType.DMA((6 + 2 * GDEV,)),
            ],
        ),
        out_shape=[
            shape((2 * pairs, rows, span), BF),
            shape((rows, width), F32),
            shape((rows, width), BF),
            shape((conts, width), BF),
            shape((conts, width), BF),
            shape((PROMPT, width), BF),
            shape((PROMPT, width), BF),
            shape((rows, width), BF),
            shape((rows // 2, width), BF),
            shape((rows // 2, width), BF),
            shape((D, units // 2), BF),
            shape((D, units // 2), BF),
            shape((width // 2, D), BF),
            shape((width // 2, D), BF),
            shape((1, shared), F32),
        ],
        compiler_params=pltpu.CompilerParams(vmem_limit_bytes=56 << 20, collective_id=0, has_side_effects=True),
        cost_estimate=pl.CostEstimate(flops=20 * 10**9, bytes_accessed=60 * 10**6, transcendentals=0),
        name="attend",
    )(starts, gaps, seg, rate, hid, vec, wq, wk, wv, w1, wo, vec)


CHUNKS = 9
IN_FIRST = 5


def reducer_scratch(count, block, cut):
    return [
        pltpu.VMEM((count, 2, 2, 2, block, cut), BF),
        pltpu.VMEM((count, 2, 2, 2, block, cut), BF),
        pltpu.VMEM((count, 2, 2, block, cut), BF),
        pltpu.VMEM((count, 2, 2, block, cut), BF),
        pltpu.VMEM((count, 2, block, cut), BF),
        pltpu.VMEM((count, 2, block, cut), BF),
        pltpu.VMEM((count, block, cut), BF),
        pltpu.SemaphoreType.DMA((4 * count,)),
        pltpu.SemaphoreType.DMA((4 * count,)),
        pltpu.SemaphoreType.DMA((count,)),
    ]


def reducer(packed, device, side, count, top, refs, done):
    held, got0, got1, held1, got2, held2, got3, sems_a, sems_b, sems_l = refs
    bit = [(device // (1 << b)) % 2 for b in range(4)]
    peers = [{"dp": bit_peer(device, b), "tensor": side} for b in range(4)]
    cut = held.shape[-1]

    def either(c, act):
        if isinstance(c, int):
            act(c % 2)
            return
        for odd in range(2):
            @pl.when(c % 2 == odd)
            def _():
                act(odd)

    def passing(c, stage, source, target, peer):
        return pltpu.make_async_remote_copy(
            src_ref=source,
            dst_ref=target,
            send_sem=sems_a.at[4 * c + stage],
            recv_sem=sems_b.at[4 * c + stage],
            device_id=peer,
            device_id_type=MESH,
        )

    def columns_of(c, first):
        at = (first - c) * cut
        return pl.ds(at if isinstance(c, int) else pl.multiple_of(at, 128), cut)

    def own_half(c):
        return pltpu.make_async_copy(packed.at[:, :, :, bit[0], :, columns_of(c, top)], held.at[c], sems_l.at[c])

    def stage0(c):
        return passing(c, 0, packed.at[:, :, :, 1 - bit[0], :, columns_of(c, top)], got0.at[c], peers[0])

    def stage1(c, odd):
        if odd:
            return passing(c, 1, held.at[c, :, 1 - bit[2]], got1.at[c], peers[2])
        return passing(c, 1, held.at[c, :, :, 1 - bit[1]], got1.at[c], peers[1])

    def stage2(c, odd):
        b = 1 if odd else 2
        return passing(c, 2, held1.at[c, :, 1 - bit[b]], got2.at[c], peers[b])

    def stage3(c):
        return passing(c, 3, held2.at[c, 1 - bit[3]], got3.at[c], peers[3])

    def begin(c):
        own_half(c).start()
        stage0(c).start()

    def after0(c):
        own_half(c).wait()
        stage0(c).wait_recv()
        held[c] = held[c] + got0[c]
        either(c, lambda odd: stage1(c, odd).start())

    def after1(c):
        def act(odd):
            stage1(c, odd).wait_recv()
            kept = held[c, :, bit[2]] if odd else held[c, :, :, bit[1]]
            held1[c] = kept + got1[c]
            stage2(c, odd).start()

        either(c, act)

    def after2(c):
        def act(odd):
            stage2(c, odd).wait_recv()
            held2[c] = held1[c, :, bit[1 if odd else 2]] + got2[c]

        either(c, act)
        stage3(c).start()

    def after3(c):
        stage3(c).wait_recv()
        done[:, columns_of(c, count - 1)] = held2[c, bit[3]] + got3[c]

    def settle():
        for c in range(count):
            for copy in (stage0(c), stage1(c, c % 2), stage2(c, c % 2), stage3(c)):
                copy.wait_send()

    return begin, after0, after1, after2, after3, settle


def bwd_kernel(
    fused, q_ref, kp_ref, vp_ref, ko_ref, vo_ref, o_ref, li_ref, e_ref, g_mine, g_theirs, out_half, *refs
):
    packed = refs[0] if fused else None
    refs = refs[1:] if fused else refs
    dq_ref, dko_ref, dvo_ref, sum_k, sum_v, relay_out, out_got = refs[:7]
    done_out, other_out = refs[7:9] if fused else (None, None)
    refs = refs[9:] if fused else refs[7:]
    dk_s, dv_s, g_s, grad_s, near_s, relay_s, far_s, sems_a, sems_b, loc_sems = refs[:10]
    pair = pl.program_id(0)
    step = pl.program_id(1)
    device = lax.axis_index("dp")
    side = lax.axis_index("tensor")
    member = device % GDEV
    rows, width = g_s.shape
    n_pairs = width // 128
    conts = rows - CHUNK
    half_p, half_c = CHUNK // 2, conts // 2
    near = {"dp": bit_peer(device, 0), "tensor": side}
    far = {"dp": bit_peer(device, 1), "tensor": side}
    across = {"dp": device, "tensor": 1 - side}
    lanes = pl.ds(pl.multiple_of(pair * 128, 128), 128)
    mine_p = pl.ds(pl.multiple_of(side * half_p, 128), half_p)
    mine_c = pl.ds(pl.multiple_of(CHUNK + side * half_c, 128), half_c)

    def remote(i, src, dst, peer):
        return pltpu.make_async_remote_copy(
            src_ref=src, dst_ref=dst, send_sem=sems_a.at[i], recv_sem=sems_b.at[i], device_id=peer, device_id_type=MESH
        )

    def heads():
        return [
            remote(0, g_theirs.at[pl.ds(0, half_p), :], g_s.at[mine_p, :], across),
            remote(1, g_theirs.at[pl.ds(half_p, half_c), :], g_s.at[mine_c, :], across),
            remote(2, out_half, out_got, across),
        ]

    def local():
        return [
            pltpu.make_async_copy(g_mine.at[pl.ds(0, half_p), :], g_s.at[mine_p, :], loc_sems.at[0]),
            pltpu.make_async_copy(g_mine.at[pl.ds(half_p, half_c), :], g_s.at[mine_c, :], loc_sems.at[1]),
        ]

    def cores(p):
        part = pl.ds(p * 128, 128)
        return remote(3 + 2 * p, grad_s.at[:, :, 1, :, part], near_s.at[:, :, :, part], near)

    def chips(p):
        part = pl.ds(p * 128, 128)
        return remote(4 + 2 * p, relay_s.at[:, :, part], far_s.at[:, :, part], far)

    if fused:
        *early_refs, done_s, other_a, early_sems = refs[10:]
        begin, after0, after1, after2, after3, settle = reducer(packed, device, side, IN_FIRST, CHUNKS - 1, early_refs, done_s)
        span_e = packed.shape[-1] // CHUNKS
        peers = [{"dp": bit_peer(device, b), "tensor": side} for b in range(4)]
        sent_e = (IN_FIRST - 1) * span_e
        swap = pltpu.make_async_remote_copy(
            src_ref=done_s.at[:, pl.ds(span_e, sent_e)],
            dst_ref=other_a,
            send_sem=early_sems.at[0],
            recv_sem=early_sems.at[1],
            device_id=across,
            device_id_type=MESH,
        )
        tick = pair * pl.num_programs(1) + step

    @pl.when((pair == 0) & (step == 0))
    def _():
        greet([near, far, across] + (peers[2:] if fused else []))
        for copy in heads() + local():
            copy.start()
        for copy in local():
            copy.wait()

    if fused:
        for late, act in ((0, begin), (1, after0), (3, after1), (5, after2), (6, after3)):
            since = tick - late
            @pl.when((since >= 0) & (since % 2 == 0) & (since // 2 < IN_FIRST))
            def _():
                act(since // 2)

        @pl.when(tick == 12)
        def _():
            swap.start()

    @pl.when((pair == 0) & (step == 1 - side))
    def _():
        heads()[0].wait_recv()

    @pl.when((pair == 0) & (step == 3 - side))
    def _():
        heads()[1].wait_recv()

    low = low_half(TILE)
    g = g_s[pl.ds(pl.multiple_of(step * TILE, TILE), TILE), lanes].astype(F32) * li_ref[...]
    prod = g * o_ref[...].astype(F32)
    zf = jnp.zeros((TILE, 128), F32)
    deltas = [
        jnp.sum(jnp.where(low, prod, zf), axis=1, keepdims=True),
        jnp.sum(jnp.where(low, zf, prod), axis=1, keepdims=True),
    ]
    gs = [jnp.where(low, g, zf).astype(BF), jnp.where(low, zf, g).astype(BF)]
    gt = jnp.transpose(g).astype(BF)
    qt = jnp.transpose(q_ref[...].astype(F32)).astype(BF)

    def grads(dq, keys, vals, at, width):
        out, dks, dvs = [], [], []
        for h in range(2):
            e = e_ref[h, :, pl.ds(at, width)]
            dp = dot_nt(gs[h], vals)
            ds = (e.astype(F32) * (dp - deltas[h])).astype(BF)
            out.append(dq[h] + dot_nn(ds, keys))
            dks.append(dot_nn(qt[h * HD : (h + 1) * HD, :], ds))
            dvs.append(dot_nn(gt[h * HD : (h + 1) * HD, :], e))
        return tuple(out), dks, dvs

    @pl.when(step == 0)
    def _():
        dk_s[...] = jnp.zeros_like(dk_s)
        dv_s[...] = jnp.zeros_like(dv_s)

    def add(at, width, dks, dvs):
        for h in range(2):
            dk_s[h * HD : (h + 1) * HD, pl.ds(at, width)] += dks[h]
            dv_s[h * HD : (h + 1) * HD, pl.ds(at, width)] += dvs[h]

    def scaled(dq):
        return (jnp.where(low, dq[0], dq[1]).astype(BF).astype(F32) * 0.125).astype(BF)

    @pl.when(step < PTILES)
    def _():
        def one(j, dq):
            at = pl.multiple_of(xor_bits(j, member) * CHUNK, CHUNK)
            dq, dks, dvs = grads(dq, kp_ref[pl.ds(at, CHUNK), :], vp_ref[pl.ds(at, CHUNK), :], at, CHUNK)
            add(at, CHUNK, dks, dvs)
            return dq

        dq_ref[...] = scaled(lax.fori_loop(0, member + 1, one, (zf, zf)))
        dko_ref[...] = jnp.zeros_like(dko_ref)
        dvo_ref[...] = jnp.zeros_like(dvo_ref)

    @pl.when(step >= PTILES)
    def _():
        dq = (zf, zf)
        for j in range(GDEV):
            span = slice(j * CHUNK, (j + 1) * CHUNK)
            dq, dks, dvs = grads(dq, kp_ref[span, :], vp_ref[span, :], j * CHUNK, CHUNK)
            add(j * CHUNK, CHUNK, dks, dvs)
        dq, dks, dvs = grads(dq, ko_ref[...], vo_ref[...], PROMPT, CONT)
        dq_ref[...] = scaled(dq)
        dko_ref[...] = jnp.transpose(jnp.concatenate(dks, axis=0)).astype(BF)
        dvo_ref[...] = jnp.transpose(jnp.concatenate(dvs, axis=0)).astype(BF)

    end = pl.num_programs(1) - 1

    @pl.when(step == end)
    def _():
        for j in range(GDEV):
            span = slice(j * CHUNK, (j + 1) * CHUNK)
            grad_s[0, j // 2, j % 2, :, lanes] = jnp.transpose(dk_s[:, span]).astype(BF)
            grad_s[1, j // 2, j % 2, :, lanes] = jnp.transpose(dv_s[:, span]).astype(BF)

    for p in range(n_pairs):
        @pl.when((pair == p) & (step == end))
        def _():
            cores(p).start()

        if p + 1 < n_pairs:
            @pl.when((pair == p + 1) & (step == 2))
            def _():
                part = pl.ds(p * 128, 128)
                cores(p).wait_recv()
                relay_s[:, :, part] = (
                    grad_s[:, 1, 0, :, part].astype(F32) + near_s[:, 1, :, part].astype(F32)
                ).astype(BF)
                chips(p).start()

    @pl.when((pair == n_pairs - 1) & (step == end))
    def _():
        last = n_pairs - 1
        sums = (sum_k, sum_v)
        for p in range(last):
            part = pl.ds(p * 128, 128)
            chips(p).wait_recv()
            for i in range(2):
                sums[i][:, part] = (
                    grad_s[i, 0, 0, :, part].astype(F32) + near_s[i, 0, :, part].astype(F32) + far_s[i, :, part].astype(F32)
                ).astype(BF)
        part = pl.ds(last * 128, 128)
        cores(last).wait_recv()
        for i in range(2):
            relay_out[i] = (grad_s[i, 1, 0, :, part].astype(F32) + near_s[i, 1, :, part].astype(F32)).astype(BF)
            sums[i][:, part] = (grad_s[i, 0, 0, :, part].astype(F32) + near_s[i, 0, :, part].astype(F32)).astype(BF)
        if fused:
            swap.wait_recv()
            done_out[...] = done_s[:, pl.ds(0, span_e)]
            other_out[...] = other_a[...]
            settle()
            swap.wait_send()
        heads()[2].wait_recv()
        for copy in heads():
            copy.wait_send()
        for p in range(n_pairs):
            cores(p).wait_send()
            if p < last:
                chips(p).wait_send()


def attend_back(q, k, v, kp, vp, o, li, e, g_mine, g_theirs, out_half, packed):
    rows, width = q.shape
    pairs = width // 128
    span = PROMPT + CONT
    tile = pl.BlockSpec((TILE, 128), lambda a, t: (t, a))
    whole = pl.BlockSpec((PROMPT, 128), lambda a, t: (0, a))
    own = pl.BlockSpec((TILE, 128), lambda a, t: (jnp.maximum(t - PTILES, 0), a))
    vmem = pl.BlockSpec(memory_space=pltpu.VMEM)
    hbm = pl.BlockSpec(memory_space=pl.ANY)
    shape = jax.ShapeDtypeStruct
    copies = 3 + 2 * pairs
    fused = packed is not None
    more_in, more_out, more_scratch = [], [], []
    if fused:
        block, cut = packed.shape[-2], packed.shape[-1] // CHUNKS
        more_in = [packed]
        more_out = [shape((block, cut), BF), shape((block, (IN_FIRST - 1) * cut), BF)]
        more_scratch = reducer_scratch(IN_FIRST, block, cut) + [
            pltpu.VMEM((block, IN_FIRST * cut), BF),
            pltpu.VMEM((block, (IN_FIRST - 1) * cut), BF),
            pltpu.SemaphoreType.DMA((2,)),
        ]
    return pl.pallas_call(
        functools.partial(bwd_kernel, fused),
        grid=(pairs, rows // TILE),
        in_specs=[tile, whole, whole, own, own, tile, tile, pl.BlockSpec((2, TILE, span), lambda a, t: (a, t, 0))]
        + [hbm] * (3 + len(more_in)),
        out_specs=[tile, tile, tile, vmem, vmem, vmem, hbm] + [vmem] * len(more_out),
        out_shape=[
            shape((rows, width), BF),
            shape((rows, width), BF),
            shape((rows, width), BF),
            shape((CHUNK, width), BF),
            shape((CHUNK, width), BF),
            shape((2, CHUNK, 128), BF),
            shape(out_half.shape, BF),
        ]
        + more_out,
        scratch_shapes=[
            pltpu.VMEM((128, PROMPT), F32),
            pltpu.VMEM((128, PROMPT), F32),
            pltpu.VMEM((rows, width), BF),
            pltpu.VMEM((2, 2, 2, CHUNK, width), BF),
            pltpu.VMEM((2, 2, CHUNK, width), BF),
            pltpu.VMEM((2, CHUNK, width), BF),
            pltpu.VMEM((2, CHUNK, width), BF),
            pltpu.SemaphoreType.DMA((copies,)),
            pltpu.SemaphoreType.DMA((copies,)),
            pltpu.SemaphoreType.DMA((2,)),
        ]
        + more_scratch,
        compiler_params=pltpu.CompilerParams(vmem_limit_bytes=60 << 20, collective_id=2, has_side_effects=True),
        cost_estimate=pl.CostEstimate(flops=30 * 10**9, bytes_accessed=60 * 10**6, transcendentals=0),
        name="attend_back",
    )(q, kp, vp, k, v, o, li, e, g_mine, g_theirs, out_half, *more_in)


UCH = 512


def polynomial(x, terms):
    out = jnp.full_like(x, terms[0])
    for term in terms[1:]:
        out = out * x + term
    return out


def error_function(x):
    x = jnp.clip(x, -3.832506856900711, 3.832506856900711)
    square = x * x
    top = polynomial(
        square,
        (0.00022905065861350646, 0.0034082910107109506, 0.050955695062380861, 0.18520832239976145, 1.128379143519084),
    )
    bottom = polynomial(
        square,
        (
            -1.1791602954361697e-7,
            0.000023547966471313185,
            0.0010179625278914885,
            0.014070470171167667,
            0.11098505178285362,
            0.49746925110067538,
            1.0,
        ),
    )
    return x * top / bottom


def gelu_pair(v):
    phi = 0.5 + 0.5 * error_function(v * 0.7071067811865476)
    density = jnp.exp(-0.5 * v * v) * 0.3989422804014327
    return v * phi, phi + v * density


def column_sum(x):
    return jnp.sum(x, axis=0, keepdims=True)


def mid_kernel(
    att_m, att_o, vec_all, vec_got, hid_all, cot_all, w1_own, w1_got, w1_swap, wo_own, wo_got, wo_swap, w2_own,
    out_ref, gatt_m, gatt_o, gmix_ref, packed, su_ref, sw_ref, sd_ref, ext_ref,
    vec_u, vec_w, w1, w2, wo, act_s, shp_s, dg_s, wide_s, acc_s, gmid_s, sub_s, mid_s, low_s, midt_s, cott_s, stage, hid, cot, sems, out_sems, send_sems, recv_sems,
):
    device = lax.axis_index("dp")
    side = lax.axis_index("tensor")
    core = device % 2
    near = {"dp": bit_peer(device, 0), "tensor": side}
    across = {"dp": device, "tensor": 1 - side}
    units = w1_own.shape[1]
    width = wo_own.shape[0]
    rows = hid.shape[0]
    full = 2 * units
    half = units // 2
    half_w = width // 2
    here_u = pl.multiple_of(units + core * half, 128)
    there_u = pl.multiple_of(units + (1 - core) * half, 128)
    here_w = pl.multiple_of(width + core * half_w, 64)
    there_w = pl.multiple_of(width + (1 - core) * half_w, 64)
    prompt, conts = CHUNK // 2, (hid_all.shape[0] - CHUNK) // 2
    own_p = pl.ds(pl.multiple_of(side * prompt, 128), prompt)
    own_c = pl.ds(pl.multiple_of(CHUNK + side * conts, 128), conts)
    at_own = 2 * D + 2 * width
    vec_own = vec_all.at[:, pl.ds(at_own, 3 * units + 2 * width)]
    vec_d = vec_all.at[:, pl.ds(at_own + 3 * units + 2 * width, 4 * D)]
    rows_in = []
    for i, (all_rows, held) in enumerate(((hid_all, hid), (cot_all, cot))):
        for j, (span, at, size) in enumerate(((own_p, 0, prompt), (own_c, prompt, conts))):
            copy = pltpu.make_async_copy(all_rows.at[span, :], held.at[pl.ds(at, size), :], sems.at[7 + 2 * i + j])
            copy.start()
            rows_in.append(copy)
    loads = []
    for i, (src, dst) in enumerate(
        [
            (wo_own, wo.at[pl.ds(0, width), :]),
            (wo_got, wo.at[pl.ds(here_w, half_w), :]),
            (wo_swap, wo.at[pl.ds(there_w, half_w), :]),
            (w1_own, w1.at[:, pl.ds(0, units)]),
            (w1_got, w1.at[:, pl.ds(here_u, half)]),
            (w1_swap, w1.at[:, pl.ds(there_u, half)]),
            (w2_own, w2.at[pl.ds(0, units), :]),
        ]
    ):
        copy = pltpu.make_async_copy(src, dst, sems.at[i])
        copy.start()
        loads.append(copy)

    piece = half // 2
    greet([near, across])

    def remote(i, src, dst, peer):
        return pltpu.make_async_remote_copy(
            src_ref=src, dst_ref=dst, send_sem=send_sems.at[i], recv_sem=recv_sems.at[i], device_id=peer, device_id_type=MESH
        )

    over, passed = [], []
    for i in range(2):
        from_own = pl.ds(pl.multiple_of(core * half + i * piece, 128), piece)
        landed = w2.at[pl.ds(pl.multiple_of(units + core * half + i * piece, 128), piece), :]
        over.append(remote(i, w2_own.at[from_own, :], landed, across))
        passed.append(remote(2 + i, landed, landed, near))
        over[i].start()

    for i in range(3):
        for j, vec in enumerate((vec_own, vec_got)):
            vec_u[i : i + 1, pl.ds(j * units, units)] = vec[0:1, pl.ds(i * units, units)]
    for i in range(2):
        for j, vec in enumerate((vec_own, vec_got)):
            vec_w[i : i + 1, pl.ds(j * width, width)] = vec[0:1, pl.ds(3 * units + i * width, width)]

    a0 = att_m[...].astype(F32)
    a1 = att_o[...].astype(F32)
    center = (jnp.sum(a0, axis=1, keepdims=True) + jnp.sum(a1, axis=1, keepdims=True)) * (1.0 / D)
    square = (jnp.sum(a0 * a0, axis=1, keepdims=True) + jnp.sum(a1 * a1, axis=1, keepdims=True)) * (1.0 / D)
    sub_scale = lax.rsqrt(square - center * center + EPSILON)
    sub_s[:, 0:width] = (a0 - center) * sub_scale
    sub_s[:, width : 2 * width] = (a1 - center) * sub_scale
    sub_gain = vec_w[0:1, :]
    low_s[...] = (sub_s[...] * sub_gain + vec_w[1:2, :]).astype(BF)
    for copy in loads[0:3] + rows_in:
        copy.wait()
    mixed = hid[...].astype(F32) + (dot_nn(low_s[...], wo[...]) + vec_d[0:1, pl.ds(0, D)])
    wide_s[...] = mixed
    mean = jnp.mean(mixed, axis=1, keepdims=True)
    mid_scale = lax.rsqrt(jnp.mean(mixed * mixed, axis=1, keepdims=True) - mean * mean + EPSILON)
    mid_s[...] = (mixed - mean) * mid_scale
    mid_gain = vec_d[0:1, pl.ds(768, D)]
    mid_full = mid_s[...] * mid_gain + vec_d[0:1, pl.ds(1536, D)]
    mid_low = mid_full.astype(BF)
    midt_s[...] = jnp.transpose(mid_full).astype(BF)
    cot_full = cot[...].astype(F32)
    cott_s[...] = jnp.transpose(cot_full).astype(BF)
    sd_ref[...] = jnp.zeros_like(sd_ref)
    sd_ref[3:4, :] = column_sum(cot_full)
    for copy in loads[3:6]:
        copy.wait()

    def lanes_sum(x):
        total = x[:, 0:128]
        for i in range(1, x.shape[1] // 128):
            total = total + x[:, i * 128 : (i + 1) * 128]
        return total

    def first(c, carry):
        at = pl.multiple_of(c * UCH, UCH)
        inner = dot_nn(mid_low, w1[:, pl.ds(at, UCH)]) + vec_u[2:3, pl.ds(at, UCH)]
        act, slope = gelu_pair(inner)
        act_s[:, pl.ds(at, UCH)] = act
        dg_s[:, pl.ds(at, UCH)] = slope.astype(BF)
        return carry[0] + lanes_sum(act), carry[1] + lanes_sum(act * act)

    zero = jnp.zeros((rows, 128), F32)
    act_sum, act_square = lax.fori_loop(0, full // UCH, first, (zero, zero))
    ffn_center = jnp.sum(act_sum, axis=1, keepdims=True) * (1.0 / full)
    ffn_scale = lax.rsqrt(
        jnp.sum(act_square, axis=1, keepdims=True) * (1.0 / full) - ffn_center * ffn_center + EPSILON
    )
    loads[6].wait()
    over[0].wait_recv()
    passed[0].start()
    acc_s[...] = jnp.zeros_like(acc_s)
    per = units // UCH
    wide = 2 * units + width

    def column_of(c, extra):
        return pl.multiple_of((c // per) * wide + lax.rem(c, per) * UCH + extra, 128)

    def send(slot, column):
        return pltpu.make_async_copy(stage.at[slot], packed.at[:, pl.ds(column, UCH)], out_sems.at[slot])

    def put(c, value, extra):
        slot = lax.rem(c, 2)

        @pl.when(c >= 2)
        def _():
            send(slot, column_of(c - 2, extra)).wait()

        stage[slot] = value
        send(slot, column_of(c, extra)).start()

    def drain(extra):
        for c in range(full // UCH - 2, full // UCH):
            send(c % 2, column_of(c, extra)).wait()

    def second(c, carry):
        at = pl.multiple_of(c * UCH, UCH)
        unit = (act_s[:, pl.ds(at, UCH)] - ffn_center) * ffn_scale
        act_s[:, pl.ds(at, UCH)] = unit
        gain = vec_u[0:1, pl.ds(at, UCH)]
        low = (unit * gain + vec_u[1:2, pl.ds(at, UCH)]).astype(BF)
        acc_s[...] += dot_nn(low, w2[pl.ds(at, UCH), :])
        grad = dot_nt(cot[...], w2[pl.ds(at, UCH), :])
        cross = grad * unit
        su_ref[0:1, pl.ds(at, UCH)] = column_sum(cross)
        su_ref[1:2, pl.ds(at, UCH)] = column_sum(grad)
        shaped = grad * gain
        shp_s[:, pl.ds(at, UCH)] = shaped
        put(c, dot_nn(cott_s[...], low).astype(BF), units)
        return carry[0] + lanes_sum(shaped), carry[1] + lanes_sum(shaped * unit)

    su_ref[...] = jnp.zeros_like(su_ref)
    sums = lax.fori_loop(0, per, second, (zero, zero))
    over[1].wait_recv()
    passed[1].start()
    for copy in passed:
        copy.wait_recv()
    s_sum, s_cross = lax.fori_loop(per, 2 * per, second, sums)
    drain(units)
    shaped_mean = jnp.sum(s_sum, axis=1, keepdims=True) * (1.0 / full)
    cross_mean = jnp.sum(s_cross, axis=1, keepdims=True) * (1.0 / full)
    out_ref[...] = (wide_s[...] + (acc_s[...] + vec_d[0:1, pl.ds(2304, D)])).astype(BF)
    gmid_s[...] = jnp.zeros_like(gmid_s)

    def third(c, carry):
        at = pl.multiple_of(c * UCH, UCH)
        g = ffn_scale * (shp_s[:, pl.ds(at, UCH)] - shaped_mean - act_s[:, pl.ds(at, UCH)] * cross_mean)
        low = (g * dg_s[:, pl.ds(at, UCH)].astype(F32)).astype(BF)
        su_ref[2:3, pl.ds(at, UCH)] = column_sum(low.astype(F32))
        gmid_s[...] += dot_nt(low, w1[:, pl.ds(at, UCH)])
        put(c, dot_nn(midt_s[...], low).astype(BF), 0)
        return carry

    lax.fori_loop(0, full // UCH, third, 0)
    drain(0)

    grad_mid = gmid_s[...]
    unit = mid_s[...]
    sd_ref[1:2, :] = column_sum(grad_mid * unit)
    sd_ref[2:3, :] = column_sum(grad_mid)
    shaped = grad_mid * mid_gain
    grad_mixed = cot[...].astype(F32) + mid_scale * (
        shaped - jnp.mean(shaped, axis=1, keepdims=True) - unit * jnp.mean(shaped * unit, axis=1, keepdims=True)
    )
    branch = grad_mixed.astype(BF)
    gmix_ref[...] = branch
    branch_f = branch.astype(F32)
    sd_ref[0:1, :] = column_sum(branch_f)
    out_grad = dot_nn(jnp.transpose(branch_f).astype(BF), low_s[...]).astype(BF)
    stage[0, :, 0:width] = out_grad[:, 0:width]
    stage[1, :, 0:width] = out_grad[:, width : 2 * width]
    last = [
        pltpu.make_async_copy(stage.at[i, :, pl.ds(0, width)], packed.at[:, pl.ds(i * wide + 2 * units, width)], out_sems.at[i])
        for i in range(2)
    ]
    for copy in last:
        copy.start()
    grad_sub = dot_nt(branch, wo[...])
    unit = sub_s[...]
    cross = grad_sub * unit
    sw_ref[...] = jnp.zeros_like(sw_ref)
    sw_ref[0:1, :] = column_sum(cross)
    sw_ref[1:2, :] = column_sum(grad_sub)
    shaped = grad_sub * sub_gain
    grad_att = sub_scale * (
        shaped - jnp.mean(shaped, axis=1, keepdims=True) - unit * jnp.mean(shaped * unit, axis=1, keepdims=True)
    )
    gatt_m[...] = grad_att[:, 0:width].astype(BF)
    gatt_o[...] = grad_att[:, width : 2 * width].astype(BF)
    parts = ext_ref.shape[0]
    if parts > 1:
        sums_u, sums_w, sums_d = su_ref[...], sw_ref[...], sd_ref[...]
        for i in range(parts):
            ext_ref[i] = jnp.concatenate(
                [
                    window(sums_u, i * (units // parts)),
                    window(sums_u, units + i * (units // parts)),
                    window(sums_w, i * (width // parts)),
                    window(sums_w, width + i * (width // parts)),
                    window(sums_d, i * (D // parts)),
                    jnp.zeros((8, 128), F32),
                ],
                axis=0,
            ).astype(BF)
    for copy in last:
        copy.wait()
    for copy in over + passed:
        copy.wait_send()


def window(rows8, start):
    base = start // 128 * 128
    size = min(256, rows8.shape[1] - base)
    view = rows8[:, base : base + size]
    shift = start - base
    if shift:
        view = pltpu.roll(view, size - shift, 1)
    return view[:, 0:128]


def middle(att_m, att_o, hid, cot, vec_all, vec_got, w1, w2, wo, parts):
    rows = att_m.shape[0]
    units = w2.shape[0]
    width = wo[0].shape[0]
    vmem = pl.BlockSpec(memory_space=pltpu.VMEM)
    hbm = pl.BlockSpec(memory_space=pl.ANY)
    shape = jax.ShapeDtypeStruct
    return pl.pallas_call(
        mid_kernel,
        in_specs=[vmem] * 4 + [hbm] * 9,
        out_specs=[vmem] * 4 + [hbm] + [vmem] * 4,
        out_shape=[
            shape((rows, D), BF),
            shape((rows, width), BF),
            shape((rows, width), BF),
            shape((rows, D), BF),
            shape((D, 2 * (2 * units + width)), BF),
            shape((8, 2 * units), F32),
            shape((8, 2 * width), F32),
            shape((8, D), F32),
            shape((parts, 48, 128), BF),
        ],
        scratch_shapes=[
            pltpu.VMEM((8, 2 * units), F32),
            pltpu.VMEM((8, 2 * width), F32),
            pltpu.VMEM((D, 2 * units), BF),
            pltpu.VMEM((2 * units, D), BF),
            pltpu.VMEM((2 * width, D), BF),
            pltpu.VMEM((rows, 2 * units), F32),
            pltpu.VMEM((rows, 2 * units), F32),
            pltpu.VMEM((rows, 2 * units), BF),
            pltpu.VMEM((rows, D), F32),
            pltpu.VMEM((rows, D), F32),
            pltpu.VMEM((rows, D), F32),
            pltpu.VMEM((rows, 2 * width), F32),
            pltpu.VMEM((rows, D), F32),
            pltpu.VMEM((rows, 2 * width), BF),
            pltpu.VMEM((D, rows), BF),
            pltpu.VMEM((D, rows), BF),
            pltpu.VMEM((2, D, UCH), BF),
            pltpu.VMEM((rows, D), BF),
            pltpu.VMEM((rows, D), BF),
            pltpu.SemaphoreType.DMA((11,)),
            pltpu.SemaphoreType.DMA((2,)),
            pltpu.SemaphoreType.DMA((4,)),
            pltpu.SemaphoreType.DMA((4,)),
        ],
        compiler_params=pltpu.CompilerParams(vmem_limit_bytes=62 << 20, collective_id=3, has_side_effects=True),
        cost_estimate=pl.CostEstimate(flops=21 * 10**9, bytes_accessed=30 * 10**6, transcendentals=0),
        name="middle",
    )(att_m, att_o, vec_all, vec_got, hid, cot, *w1, *wo, w2)


def final_kernel(
    bits, hid, vec_all, dq, dk, dv, wq, wk, wv, gmix, ext, sum_k, sum_v, relay, first_done, first_other, packed,
    gin, late_out, vec_out, early_out,
    loc_s, far_s, unit_s, mine_s, norm_s, send_c, recv_c, send_p, recv_p, give_c, give_p, late_s, small_s,
    vec_s, vec_r, done_s, other_b, sems_a, sems_b, loc_sems, *stage_refs,
):
    device = lax.axis_index("dp")
    side = lax.axis_index("tensor")
    across = {"dp": device, "tensor": 1 - side}
    peers = [{"dp": bit_peer(device, b), "tensor": side} for b in range(bits)]
    rows, width = dq.shape
    prompt = sum_k.shape[0]
    conts = rows - prompt
    half_p, half_c = prompt // 2, conts // 2
    own_p = pl.multiple_of(side * half_p, 128)
    their_p = pl.multiple_of((1 - side) * half_p, 128)
    own_c = pl.multiple_of(prompt + side * half_c, 128)
    their_c = pl.multiple_of(prompt + (1 - side) * half_c, 128)
    lanes = 3 * width + 128

    greet(peers + [across])
    count = [0]

    def remote(src, dst, peer):
        i = count[0]
        count[0] += 1
        copy = pltpu.make_async_remote_copy(
            src_ref=src, dst_ref=dst, send_sem=sems_a.at[i], recv_sem=sems_b.at[i], device_id=peer, device_id_type=MESH
        )
        copy.start()
        return copy

    share = remote(relay, far_s, peers[1])

    in_last = CHUNKS - IN_FIRST
    begin, after0, after1, after2, after3, settle = reducer(packed, device, side, in_last, in_last - 1, stage_refs[-10:], done_s)
    cut = packed.shape[-1] // CHUNKS
    half_cut = cut // 2
    swap_e = remote(first_done.at[:, pl.ds(half_cut, half_cut)], other_b, across)

    def each(act):
        for c in range(in_last):
            act(c)

    each(begin)

    gain_f = vec_all[:, pl.ds(0, D)]
    bias_f = vec_all[:, pl.ds(D, D)]

    def unit_rows(at, size):
        x = hid[pl.ds(at, size), :].astype(F32)
        center = jnp.mean(x, axis=1, keepdims=True)
        scale = lax.rsqrt(jnp.mean(x * x, axis=1, keepdims=True) - center * center + EPSILON)
        return (x - center) * scale, scale

    def part_of(at, size, k_rows, v_rows):
        return dot_nt(dq[pl.ds(at, size), :], wq[...]) + dot_nt(k_rows, wk[...]) + dot_nt(v_rows, wv[...])

    def gather(part, unit):
        return column_sum(part * unit), column_sum(part)

    def normed_rows(at, size, unit):
        norm_s[:, pl.ds(at, size)] = jnp.transpose(unit * gain_f + bias_f).astype(BF)

    part = part_of(their_c, half_c, dk[pl.ds(their_c, half_c), :], dv[pl.ds(their_c, half_c), :])
    send_c[...] = part.astype(BF)
    y_cont = remote(send_c, recv_c, across)
    unit, _ = unit_rows(their_c, half_c)
    gain_grad, bias_grad = gather(part, unit)
    normed_rows(their_c, half_c, unit)
    unit, scale_c = unit_rows(own_c, half_c)
    part = part_of(own_c, half_c, dk[pl.ds(own_c, half_c), :], dv[pl.ds(own_c, half_c), :])
    mine_s[pl.ds(half_p, half_c), :] = part
    unit_s[pl.ds(half_p, half_c), :] = unit
    g, b = gather(part, unit)
    gain_grad, bias_grad = gain_grad + g, bias_grad + b
    normed_rows(own_c, half_c, unit)

    each(after0)
    share.wait_recv()
    for i, total in enumerate((sum_k, sum_v)):
        loc_s[i, :, pl.ds(0, width - 128)] = total[:, pl.ds(0, width - 128)]
        loc_s[i, :, pl.ds(width - 128, 128)] = (
            total[:, pl.ds(width - 128, 128)].astype(F32) + far_s[i].astype(F32)
        ).astype(BF)
    part = part_of(their_p, half_p, loc_s[0, pl.ds(their_p, half_p), :], loc_s[1, pl.ds(their_p, half_p), :])
    send_p[...] = part.astype(BF)
    y_prompt = remote(send_p, recv_p, across)
    unit, _ = unit_rows(their_p, half_p)
    normed_rows(their_p, half_p, unit)
    g, b = gather(part, unit)
    gain_grad, bias_grad = gain_grad + g, bias_grad + b
    unit, scale_p = unit_rows(own_p, half_p)
    unit_s[pl.ds(0, half_p), :] = unit
    normed_rows(own_p, half_p, unit)
    part = part_of(own_p, half_p, loc_s[0, pl.ds(own_p, half_p), :], loc_s[1, pl.ds(own_p, half_p), :])
    mine_s[pl.ds(0, half_p), :] = part
    g, b = gather(part, unit)
    gain_grad, bias_grad = gain_grad + g, bias_grad + b

    blocks = 1 << bits
    block = D // blocks

    def keep(value, lane):
        low = value.astype(BF)
        for i in range(blocks):
            late_s[i // 2, i % 2, :, pl.ds(lane, width)] = low[i * block : (i + 1) * block, :]

    keep(dot_nn(norm_s[...], dq[...]), 0)
    q_bias = column_sum(dq[...].astype(F32))
    for i, rest in enumerate((dk, dv)):
        keep(
            dot_nn(norm_s[:, pl.ds(0, prompt)], loc_s[i])
            + dot_nn(norm_s[:, pl.ds(prompt, conts)], rest[pl.ds(prompt, conts), :]),
            (i + 1) * width,
        )
    v_bias = column_sum(loc_s[1].astype(F32)) + column_sum(dv[pl.ds(prompt, conts), :].astype(F32))

    def norm_back(total, unit, scale, mixed):
        shaped = total * gain_f
        return mixed.astype(F32) + scale * (
            shaped - jnp.mean(shaped, axis=1, keepdims=True) - unit * jnp.mean(shaped * unit, axis=1, keepdims=True)
        )

    small_s[...] = jnp.zeros_like(small_s)
    small_s[0:1, pl.ds(0, width)] = q_bias
    small_s[1:2, pl.ds(0, width)] = v_bias
    small_s[2:3, pl.ds(0, D)] = gain_grad
    small_s[3:4, pl.ds(0, D)] = bias_grad
    small = small_s[...]
    row_id = lax.broadcasted_iota(jnp.int32, (8, 128), 0)
    for i in range(blocks):
        narrow = window(small, i * (width // blocks))
        broad = window(small, i * block)
        tail = jnp.concatenate([ext[i, pl.ds(32, 16), :].astype(F32)[0:8], jnp.where(row_id < 2, narrow, broad)], axis=0)
        late_s[i // 2, i % 2, pl.ds(0, 32), pl.ds(3 * width, 128)] = ext[i, pl.ds(0, 32), :]
        late_s[i // 2, i % 2, pl.ds(32, 16), pl.ds(3 * width, 128)] = tail.astype(BF)

    def input_rows(arrived, at, size, scale, held, rows_at, sem):
        arrived[0].wait_recv()
        here = pl.ds(at, size)
        total = mine_s[here, :] + arrived[1][...].astype(F32)
        held[...] = norm_back(total, unit_s[here, :], scale, gmix[here, :]).astype(BF)
        back = remote(held, gin.at[pl.ds(rows_at, size), :], across)
        kept = pltpu.make_async_copy(held, gin.at[pl.ds(rows_at, size), :], loc_sems.at[sem])
        kept.start()
        return back, kept

    source = late_s
    stages = []
    for bit in range(bits):
        landing, kept = stage_refs[2 * bit], stage_refs[2 * bit + 1]
        mine = (device // (1 << bit)) % 2
        copy = remote(source.at[:, 1 - mine], landing, peers[bit])
        if bit == 0:
            back_c, keep_c = input_rows((y_cont, recv_c), half_p, half_c, scale_c, give_c, own_c, 0)
        if bit == 1:
            each(after1)
            back_p, keep_p = input_rows((y_prompt, recv_p), 0, half_p, scale_p, give_p, own_p, 1)
        if bit == 2:
            each(after2)
        if bit == 3:
            each(after3)
        copy.wait_recv()
        stages.append(copy)
        for i in range(landing.shape[0]):
            kept[i // 2, i % 2] = (source[i, mine].astype(F32) + landing[i].astype(F32)).astype(BF)
        source = kept
    late_out[...] = source[0, 0, :, pl.ds(0, 3 * width)].astype(F32)
    vec_s[...] = source[0, 0, :, pl.ds(3 * width, 128)]
    swap = remote(vec_s, vec_r, across)
    swap_e.wait_recv()
    last_e = in_last * cut
    early_out[:, pl.ds(0, half_cut)] = done_s[:, pl.ds(0, half_cut)].astype(F32) + other_b[...].astype(F32)
    early_out[:, pl.ds(half_cut, last_e - half_cut)] = done_s[:, pl.ds(half_cut, last_e - half_cut)].astype(
        F32
    ) + first_other[:, pl.ds(0, last_e - half_cut)].astype(F32)
    early_out[:, pl.ds(last_e, half_cut)] = first_done[:, pl.ds(0, half_cut)].astype(F32) + first_other[
        :, pl.ds(last_e - half_cut, half_cut)
    ].astype(F32)
    settle()
    swap.wait_recv()
    vec_out[0] = vec_s[...].astype(F32)
    vec_out[1] = vec_r[...].astype(F32)
    for copy in stages + [share, swap_e, y_cont, y_prompt, swap]:
        copy.wait_send()
    for copy in (back_c, back_p):
        copy.wait_recv()
        copy.wait_send()
    keep_c.wait()
    keep_p.wait()


def finish(hid, vec_all, dq, dk, dv, wq, wk, wv, gmix, ext, sum_k, sum_v, relay, first_done, first_other, packed):
    rows, width = dq.shape
    ranks = lax.axis_size("dp")
    bits = ranks.bit_length() - 1
    block = D // ranks
    prompt = sum_k.shape[0]
    conts = rows - prompt
    lanes = 3 * width + 128
    vmem = pl.BlockSpec(memory_space=pltpu.VMEM)
    hbm = pl.BlockSpec(memory_space=pl.ANY)
    shape = jax.ShapeDtypeStruct
    copies = 7 + bits
    cut = packed.shape[-1] // CHUNKS
    stages = []
    for bit in range(bits):
        left = ranks >> (bit + 1)
        stages.append(pltpu.VMEM((left, block, lanes), BF))
        stages.append(pltpu.VMEM((max(left // 2, 1), min(left, 2), block, lanes), BF))
    return pl.pallas_call(
        functools.partial(final_kernel, bits),
        in_specs=[vmem] * 15 + [hbm],
        out_specs=[hbm, vmem, vmem, vmem],
        out_shape=[shape((rows, D), BF), shape((block, 3 * width), F32), shape((2, block, 128), F32), shape((block, packed.shape[-1] // 2), F32)],
        scratch_shapes=[
            pltpu.VMEM((2, prompt, width), BF),
            pltpu.VMEM((2, prompt, 128), BF),
            pltpu.VMEM((rows // 2, D), F32),
            pltpu.VMEM((rows // 2, D), F32),
            pltpu.VMEM((D, rows), BF),
            pltpu.VMEM((conts // 2, D), BF),
            pltpu.VMEM((conts // 2, D), BF),
            pltpu.VMEM((prompt // 2, D), BF),
            pltpu.VMEM((prompt // 2, D), BF),
            pltpu.VMEM((conts // 2, D), BF),
            pltpu.VMEM((prompt // 2, D), BF),
            pltpu.VMEM((ranks // 2, 2, block, lanes), BF),
            pltpu.VMEM((8, D + 128), F32),
            pltpu.VMEM((block, 128), BF),
            pltpu.VMEM((block, 128), BF),
            pltpu.VMEM((block, (CHUNKS - IN_FIRST) * cut), BF),
            pltpu.VMEM((block, cut // 2), BF),
            pltpu.SemaphoreType.DMA((copies,)),
            pltpu.SemaphoreType.DMA((copies,)),
            pltpu.SemaphoreType.DMA((2,)),
        ]
        + stages
        + reducer_scratch(CHUNKS - IN_FIRST, block, cut),
        compiler_params=pltpu.CompilerParams(vmem_limit_bytes=56 << 20, collective_id=1, has_side_effects=True),
        cost_estimate=pl.CostEstimate(flops=5 * 10**9, bytes_accessed=20 * 10**6, transcendentals=0),
        name="finish",
    )(hid, vec_all, dq, dk, dv, wq, wk, wv, gmix, ext, sum_k, sum_v, relay, first_done, first_other, packed)


def flip(value, axis, bit):
    return lax.ppermute(value, axis, [(i, i ^ (1 << bit)) for i in range(lax.axis_size(axis))])


def contract_rows(left, right):
    return lax.dot_general(left, right, (((0,), (0,)), ((), ())), preferred_element_type=F32)


def back_project(left, right):
    return lax.dot_general(left, right, (((1,), (1,)), ((), ())), preferred_element_type=F32)


def norm_rows(values, gain, bias):
    center = jnp.mean(values, axis=-1, keepdims=True)
    spread = jnp.mean(values * values, axis=-1, keepdims=True) - center * center
    scaled = lax.rsqrt(spread + EPSILON)
    unit_rows = (values - center) * scaled
    return (unit_rows * gain + bias, unit_rows, scaled)


def norm_back(grad_rows, gain, unit_rows, scaled):
    shaped = grad_rows * gain
    return scaled * (
        shaped
        - jnp.mean(shaped, axis=-1, keepdims=True)
        - unit_rows * jnp.mean(shaped * unit_rows, axis=-1, keepdims=True)
    )


def in_order(which, mine, other, axis):
    return jnp.where(
        which == 0,
        jnp.concatenate([mine, other], axis=axis),
        jnp.concatenate([other, mine], axis=axis),
    )


def halving(value, device):
    bits = lax.axis_size("dp").bit_length() - 1
    rows, columns = value.shape
    current = value
    for bit in range(bits):
        upper = device // (1 << bit) % 2
        left = bits - bit
        view = current.reshape((1 << (left - 1), 2, -1, columns))
        kept = lax.dynamic_index_in_dim(view, upper, 1, keepdims=False)
        sent = lax.dynamic_index_in_dim(view, 1 - upper, 1, keepdims=False)
        got = flip(sent, "dp", bit)
        current = (kept.astype(F32) + got.astype(F32)).astype(BF)
    return current.reshape(rows >> bits, columns)


def side_by_side(parts):
    total = sum(part.shape[0] for part in parts)
    row, at = jnp.zeros((1, total), F32), 0
    for part in parts:
        size = part.shape[0]
        row = row + jnp.pad(part.astype(F32)[None], ((0, 0), (at, total - at - size)))
        at += size
    return row


def half_of(value, which):
    prompt, conts = CHUNK // 2, (value.shape[0] - CHUNK) // 2
    return jnp.concatenate(
        [
            lax.dynamic_slice_in_dim(value, which * prompt, prompt),
            lax.dynamic_slice_in_dim(value, CHUNK + which * conts, conts),
        ]
    )


def joined(which, mine, other):
    prompt = CHUNK // 2
    low = jnp.where(which == 0, mine, other)
    high = jnp.where(which == 0, other, mine)
    return jnp.concatenate([low[:prompt], high[:prompt], low[prompt:], high[prompt:]])


def body(
    hidden_in,
    cotangent,
    prompt_start,
    cont_gap,
    seg_len,
    dilation_rate,
    pre_gain,
    pre_bias,
    query_weight,
    query_bias,
    key_weight,
    value_weight,
    value_bias,
    sub_gain,
    sub_bias,
    out_weight,
    out_bias,
    mid_gain,
    mid_bias,
    inner_weight,
    inner_bias,
    ffn_gain,
    ffn_bias,
    outer_weight,
    outer_bias,
):
    device = lax.axis_index("dp")
    ranks = lax.axis_size("dp")
    group_id = device // GDEV
    member = device % GDEV
    tensor_id = lax.axis_index("tensor")
    core = device % 2
    width = query_weight.shape[1]
    units = inner_weight.shape[1]
    pairs = width // 128
    rows = hidden_in.shape[0]
    prompt_rows = CHUNK
    cont_count = (rows - prompt_rows) // CONT

    vectors = side_by_side(
        [
            pre_gain,
            pre_bias,
            query_bias,
            value_bias,
            ffn_gain,
            ffn_bias,
            inner_bias,
            sub_gain,
            sub_bias,
            out_bias,
            mid_gain,
            mid_bias,
            outer_bias,
        ]
    )
    pre_gain_f = pre_gain.astype(F32)

    (
        weighed,
        inverse,
        queries,
        keys,
        values,
        prompt_keys,
        prompt_values,
        attended,
        att_mine,
        att_got,
        *pieces,
        vectors_other,
    ) = attend(
        prompt_start,
        cont_gap,
        seg_len,
        dilation_rate,
        hidden_in,
        vectors,
        query_weight,
        key_weight,
        value_weight,
        inner_weight,
        out_weight,
    )
    inner_parts = (inner_weight, pieces[0], pieces[1])
    out_parts = (out_weight, pieces[2], pieces[3])

    fused = ranks == 16
    out_half, grad_mine, grad_theirs, grad_mixed_low, packed, sum_u, sum_w, sum_d, ext = middle(
        att_mine,
        att_got,
        hidden_in,
        cotangent,
        vectors,
        vectors_other,
        inner_parts,
        outer_weight,
        out_parts,
        ranks if fused else 1,
    )

    grad_query_in, own_key_grad, own_value_grad, key_sum, value_sum, relay, out_got, *early = attend_back(
        queries,
        keys,
        values,
        prompt_keys,
        prompt_values,
        attended,
        inverse,
        weighed,
        grad_mine,
        grad_theirs,
        out_half,
        packed.reshape(2, 2, 2, 2, D // ranks, -1) if fused else None,
    )
    if not fused:
        early = lax.psum_scatter(packed, "dp", scatter_dimension=0, tiled=True)
        early_mine, early_other = jnp.split(early, 2, axis=1)
        early_sum = early_mine.astype(F32) + flip(early_other, "tensor", 0).astype(F32)
    output = joined(tensor_id, out_half, out_got)
    block = D // ranks
    per_u, per_w, per_d = units // ranks, width // ranks, D // ranks
    if fused:
        input_low, late, vec, early_sum = finish(
            hidden_in,
            vectors,
            grad_query_in,
            own_key_grad,
            own_value_grad,
            query_weight,
            key_weight,
            value_weight,
            grad_mixed_low,
            ext,
            key_sum,
            value_sum,
            relay,
            *early,
            packed.reshape(2, 2, 2, 2, D // ranks, -1),
        )
        ffn_gain_grad, ffn_bias_grad, inner_bias_grad = [vec[0, i, :per_u] + vec[1, 8 + i, :per_u] for i in range(3)]
        sub_gain_grad, sub_bias_grad = [vec[0, 16 + i, :per_w] + vec[1, 24 + i, :per_w] for i in range(2)]
        out_bias_grad, mid_gain_grad, mid_bias_grad, outer_bias_grad = [
            vec[0, 32 + i, :per_d] + vec[1, 32 + i, :per_d] for i in range(4)
        ]
        query_bias_grad, value_bias_grad = [vec[0, 40 + i, :per_w] for i in range(2)]
        pre_gain_grad, pre_bias_grad = [vec[0, 42 + i, :per_d] + vec[1, 42 + i, :per_d] for i in range(2)]
    else:
        pre_normed, pre_unit, pre_scale = norm_rows(hidden_in.astype(F32), pre_gain_f, pre_bias.astype(F32))
        pre_low = pre_normed.astype(BF)
        last = width - 128
        far = flip(relay, "dp", 1).astype(F32)
        summed = jnp.stack([key_sum, value_sum]).astype(F32)
        summed = jnp.concatenate([summed[:, :, :last], summed[:, :, last:] + far], axis=2).astype(BF)
        grad_keys = jnp.concatenate([summed[0], own_key_grad[prompt_rows:]], axis=0)
        grad_values = jnp.concatenate([summed[1], own_value_grad[prompt_rows:]], axis=0)

        query_weight_grad = contract_rows(pre_low, grad_query_in)
        key_weight_grad = contract_rows(pre_low, grad_keys)
        value_weight_grad = contract_rows(pre_low, grad_values)
        query_bias_grad = jnp.sum(grad_query_in.astype(F32), axis=0)
        value_bias_grad = jnp.sum(grad_values.astype(F32), axis=0)
        grad_normed_part = (
            back_project(grad_query_in, query_weight)
            + back_project(grad_keys, key_weight)
            + back_project(grad_values, value_weight)
        )
        grad_normed_low = grad_normed_part.astype(BF)
        grad_normed = grad_normed_low.astype(F32) + flip(grad_normed_low, "tensor", 0).astype(F32)
        pre_gain_grad = jnp.sum(grad_normed * pre_unit, axis=0)
        pre_bias_grad = jnp.sum(grad_normed, axis=0)
        grad_mixed_all = joined(tensor_id, grad_mixed_low, flip(grad_mixed_low, "tensor", 0)).astype(F32)
        input_low = (grad_mixed_all + norm_back(grad_normed, pre_gain_f, pre_unit, pre_scale)).astype(BF)

        vec = jnp.concatenate(
            [
                sum_u[:3].reshape(3, 2, ranks, per_u).transpose(2, 1, 0, 3).reshape(ranks, 6 * per_u),
                sum_w[:2].reshape(2, 2, ranks, per_w).transpose(2, 1, 0, 3).reshape(ranks, 4 * per_w),
                sum_d[:4].reshape(4, ranks, per_d).swapaxes(0, 1).reshape(ranks, 4 * per_d),
                jnp.stack([query_bias_grad, value_bias_grad]).reshape(2, ranks, per_w).swapaxes(0, 1).reshape(ranks, 2 * per_w),
                jnp.stack([pre_gain_grad, pre_bias_grad]).reshape(2, ranks, per_d).swapaxes(0, 1).reshape(ranks, 2 * per_d),
            ],
            axis=1,
        )
        count = vec.shape[1]
        vec = jnp.pad(vec, ((0, 0), (0, block * 128 - count))).reshape(D, 128)
        late = halving(
            jnp.concatenate(
                [p.astype(BF) for p in (query_weight_grad, key_weight_grad, value_weight_grad, vec)], axis=1
            ),
            device,
        )
        vec = late[:, 3 * width :].reshape(-1)[:count]
        late = late[:, : 3 * width].astype(F32)
        at_w = 6 * per_u
        at_d = at_w + 4 * per_w
        at_late = at_d + 4 * per_d
        got = flip(vec[:at_late], "tensor", 0).astype(F32)
        vec = vec.astype(F32)
        ffn_gain_grad, ffn_bias_grad, inner_bias_grad = (vec[: 3 * per_u] + got[3 * per_u : at_w]).reshape(3, per_u)
        sub_gain_grad, sub_bias_grad = (vec[at_w : at_w + 2 * per_w] + got[at_w + 2 * per_w : at_d]).reshape(2, per_w)
        out_bias_grad, mid_gain_grad, mid_bias_grad, outer_bias_grad = (vec[at_d:at_late] + got[at_d:]).reshape(4, per_d)
        query_bias_grad, value_bias_grad = vec[at_late : at_late + 2 * per_w].reshape(2, per_w)
        pre_gain_grad, pre_bias_grad = vec[at_late + 2 * per_w :].reshape(2, per_d)
    inner_weight_grad = early_sum[:, :units]
    outer_weight_grad = early_sum[:, units : 2 * units].T
    out_weight_grad = early_sum[:, 2 * units :].T
    return (
        output,
        input_low,
        pre_gain_grad,
        pre_bias_grad,
        late[:, :width],
        query_bias_grad,
        late[:, width : 2 * width],
        late[:, 2 * width : 3 * width],
        value_bias_grad,
        sub_gain_grad,
        sub_bias_grad,
        out_weight_grad,
        out_bias_grad,
        mid_gain_grad,
        mid_bias_grad,
        inner_weight_grad,
        inner_bias_grad,
        ffn_gain_grad,
        ffn_bias_grad,
        outer_weight_grad,
        outer_bias_grad,
    )

def solution(mesh):
    placed = (
        P("dp", None),
        P("dp", None),
        P(),
        P(),
        P(),
        P(),
        P(),
        P(),
        P(None, "tensor"),
        P("tensor"),
        P(None, "tensor"),
        P(None, "tensor"),
        P("tensor"),
        P("tensor"),
        P("tensor"),
        P("tensor", None),
        P(),
        P(),
        P(),
        P(None, "tensor"),
        P("tensor"),
        P("tensor"),
        P("tensor"),
        P("tensor", None),
        P(),
    )
    return jax.shard_map(
        body,
        mesh=mesh,
        in_specs=placed,
        out_specs=(
            P("dp", None),
            P("dp", None),
            P("dp"),
            P("dp"),
            P("dp", "tensor"),
            P(("tensor", "dp")),
            P("dp", "tensor"),
            P("dp", "tensor"),
            P(("tensor", "dp")),
            P(("tensor", "dp")),
            P(("tensor", "dp")),
            P("tensor", "dp"),
            P("dp"),
            P("dp"),
            P("dp"),
            P("dp", "tensor"),
            P(("tensor", "dp")),
            P(("tensor", "dp")),
            P(("tensor", "dp")),
            P("tensor", "dp"),
            P("dp"),
        ),
        check_vma=False,
    )
```

profile of v0, /device:TPU:0, one launch (start us, length us, event | category | flops | bytes accessed | tf_op | source)
XLA Modules:
  0.0 322.7 jit_solution(3383307715363969741)
XLA Ops:
  0.7 0.7 broadcast_in_dim.56
  1.4 0.7 broadcast_in_dim.57
  2.0 0.7 broadcast_in_dim.58
  2.7 0.7 broadcast_in_dim.52
  3.4 0.7 broadcast_in_dim.53
  4.1 0.7 broadcast_in_dim.61
  4.8 0.7 broadcast_in_dim.62
  5.5 0.7 broadcast_in_dim.63
  6.2 0.7 broadcast_in_dim.64
  6.8 0.7 broadcast_in_dim.54
  7.5 0.7 broadcast_in_dim.55
  8.2 0.7 broadcast_in_dim.59
  8.9 0.7 broadcast_in_dim.60
  9.6 0.7 convert_add_fusion.vec.vec_hbm.vec_all
  10.2 1.4 copy.46.seg
  11.6 1.4 copy.47.rate
  12.9 63.9 %attend.1 = (bf16[6,1280,2304]{2,1,0:T(8,128)(2,1)}, f32[1280,384]{1,0:T(8,128)}, bf16[1280,384]{1,0:T(8,128)(2,1)}, bf16[768,384]{1,0:T(8,128)(2,1)}, bf16[768,...) custom-call(s32[4]{0:T(128)} %starts.1, ...), custom_call_target="tpu_custom_call" | custom-call | flops 20000000000 | bytes 60000000 | tf_op jit(solution)/shard_map/attend/pallas_call | solution.py:396
  76.8 61.9 %middle.1 = (bf16[640,768]{1,0:T(8,128)(2,1)}, bf16[640,384]{1,0:T(8,128)(2,1)}, bf16[640,384]{1,0:T(8,128)(2,1)}, bf16[640,768]{1,0:T(8,128)(2,1)}, bf16[768,69...) custom-call(bf16[640,384]{1,0:T(8,128)(2,1)} %get-tuple-element.55.a, ...), custom_call_target="tpu_custom_call" | custom-call | flops 20999999488 | bytes 30000000 | tf_op jit(solution)/shard_map/middle/pallas_call | solution.py:1114
  138.7 107.1 %attend_back.1 = (bf16[1280,384]{1,0:T(8,128)(2,1)}, bf16[1280,384]{1,0:T(8,128)(2,1)}, bf16[1280,384]{1,0:T(8,128)(2,1)}, bf16[512,384]{1,0:T(8,128)(2,1)}, bf1...) custom-call(bf16[1280,384]{1,0:T(8,128)(2,1)} %get-tuple-element.63., ...), custom_call_target="tpu_custom_call" | custom-call | flops 30000001024 | bytes 60000000 | tf_op jit(solution)/shard_map/attend_back/pallas_call | solution.py:780
  245.9 0.0 copy-start.2
  245.9 65.1 %finish.1 = (bf16[1280,768]{1,0:T(8,128)(2,1)}, f32[48,1152]{1,0:T(8,128)}, f32[2,48,128]{2,1,0:T(8,128)}, f32[48,3456]{1,0:T(8,128)}) custom-call(bf16[1280,768]{1,0:T(8,128)(2,1)} %hid.3, f32[1,10752]{1,0:T(1,128)} %convert_add_fusion.vec.vec_hbm.vec_all, bf16[1280,384]{1,0:T(8,128)(2,1)} %get-tuple-element.75.dq, bf16[1280,384]{1,0:T(8,128)(2,1)} %get-tuple-element.76.dk, ...), custom_call_target="tpu_custom_call" | custom-call | flops 5000000000 | bytes 20000000 | tf_op jit(solution)/shard_map/finish/pallas_call | solution.py:1371
  311.0 0.0 copy-start.1
  311.0 1.8 fusion
  312.8 1.9 slice_bitcast_fusion
  314.7 1.4 add_bitcast_fusion
  316.1 1.3 add_bitcast_fusion.7
  317.4 1.3 add_bitcast_fusion.1
  318.7 0.0 copy-done.2
  318.7 0.0 copy-done.1
  318.7 0.1 broadcast_select_fusion.1
  319.0 0.0 copy-start
  319.0 1.4 pad_maximum_fusion
  320.4 0.8 copy-done
  321.3 1.3 copy.49
  (4 shorter events, 0.1 us)
Async XLA Ops:
  245.9 72.9 %copy-start.2 = (bf16[640,768]{1,0:T(8,128)(2,1)S(1)}, bf16[640,768]{1,0:T(8,128)(2,1)}, u32[]{:S(2)}) copy-start(bf16[640,768]{1,0:T(8,128)(2,1)} %get-tuple-element.74) | copy-start | bytes 2949124
  311.0 7.7 %copy-start.1 = (bf16[640,768]{1,0:T(8,128)(2,1)S(1)}, bf16[640,768]{1,0:T(8,128)(2,1)}, u32[]{:S(2)}) copy-start(bf16[640,768]{1,0:T(8,128)(2,1)} %get-tuple-element.62.out_half) | copy-start | bytes 2949124
  319.0 2.3 copy-start
where the time goes:
time: 327 us; the launch traced here: 323 us
  Pallas kernels  298 us (91%)
  local copies, waits for them, and re-layouts  17.6 us (5%)
  other arithmetic  6.19 us (2%)
    pallas_call x1, Pallas kernels, attend_back(): pl.pallas_call(functools.partial(bwd_kernel, fused), grid=(pairs, rows //...  107 us
    pallas_call x1, Pallas kernels, finish(): pl.pallas_call(functools.partial(final_kernel, bits), in_specs=[vmem] * 1...  65.1 us
    pallas_call x1, Pallas kernels, attend(): pl.pallas_call(fwd_kernel, grid_spec=pltpu.PrefetchScalarGridSpec(num_sca...  63.9 us
    pallas_call x1, Pallas kernels, middle(): pl.pallas_call(mid_kernel, in_specs=[vmem] * 4 + [hbm] * 9, out_specs=[vm...  61.9 us
    broadcast_in_dim x13, local copies, waits for them, and re-layouts, side_by_side(): part.astype(F32)[None]  8.91 us

commit v1 on v0

--- a/solution.py
+++ b/solution.py
@@ -36,17 +36,16 @@
 
 def settings(seg, rate, pair):
     def row(value):
-        return jnp.broadcast_to(value, (1, 128)).astype(F32)
+        return jnp.full((1, 128), value, jnp.int32).astype(F32)
 
     def rest(number, period):
         return number - period * jnp.floor((number + 0.5) / period)
 
-    at = pl.ds(pair, 1)
-    second, third = row(rate[at, 1:2]), row(rate[at, 2:3])
-    head = jnp.full((1, 128), 2 * pair, jnp.int32).astype(F32)
+    second, third = row(rate[1, pair]), row(rate[2, pair])
+    head = row(2 * pair)
     return (
-        1.0 / row(seg[at, 0:1]),
-        1.0 / row(seg[at, 1:2]),
+        1.0 / row(seg[0, pair]),
+        1.0 / row(seg[1, pair]),
         second,
         1.0 / second,
         third,
@@ -398,7 +397,7 @@
         grid_spec=pltpu.PrefetchScalarGridSpec(
             num_scalar_prefetch=0,
             grid=(pairs, rows // TILE),
-            in_specs=[smem] * 2 + [vmem] * 7 + [hbm] * 3,
+            in_specs=[smem] * 4 + [vmem] * 5 + [hbm] * 3,
             out_specs=[
                 pl.BlockSpec((2, TILE, span), lambda a, t: (a, t, 0)),
                 pl.BlockSpec((TILE, 128), lambda a, t: (t, a)),
@@ -441,8 +440,8 @@
     )(starts, gaps, seg, rate, hid, vec, wq, wk, wv, w1, wo, vec)
 
 
-CHUNKS = 9
-IN_FIRST = 5
+EARLY = 2
+FIRST_CUT = 1920
 
 
 def reducer_scratch(count, block, cut):
@@ -460,20 +459,11 @@
     ]
 
 
-def reducer(packed, device, side, count, top, refs, done):
+def reducer(packed, device, side, base, refs, done):
     held, got0, got1, held1, got2, held2, got3, sems_a, sems_b, sems_l = refs
     bit = [(device // (1 << b)) % 2 for b in range(4)]
     peers = [{"dp": bit_peer(device, b), "tensor": side} for b in range(4)]
     cut = held.shape[-1]
-
-    def either(c, act):
-        if isinstance(c, int):
-            act(c % 2)
-            return
-        for odd in range(2):
-            @pl.when(c % 2 == odd)
-            def _():
-                act(odd)
 
     def passing(c, stage, source, target, peer):
         return pltpu.make_async_remote_copy(
@@ -485,23 +475,24 @@
             device_id_type=MESH,
         )
 
+    count = held.shape[0]
+
     def columns_of(c, first):
-        at = (first - c) * cut
-        return pl.ds(at if isinstance(c, int) else pl.multiple_of(at, 128), cut)
+        return pl.ds(first + (count - 1 - c) * cut, cut)
 
     def own_half(c):
-        return pltpu.make_async_copy(packed.at[:, :, :, bit[0], :, columns_of(c, top)], held.at[c], sems_l.at[c])
+        return pltpu.make_async_copy(packed.at[:, :, :, bit[0], :, columns_of(c, base)], held.at[c], sems_l.at[c])
 
     def stage0(c):
-        return passing(c, 0, packed.at[:, :, :, 1 - bit[0], :, columns_of(c, top)], got0.at[c], peers[0])
-
-    def stage1(c, odd):
-        if odd:
+        return passing(c, 0, packed.at[:, :, :, 1 - bit[0], :, columns_of(c, base)], got0.at[c], peers[0])
+
+    def stage1(c):
+        if c % 2:
             return passing(c, 1, held.at[c, :, 1 - bit[2]], got1.at[c], peers[2])
         return passing(c, 1, held.at[c, :, :, 1 - bit[1]], got1.at[c], peers[1])
 
-    def stage2(c, odd):
-        b = 1 if odd else 2
+    def stage2(c):
+        b = 1 if c % 2 else 2
         return passing(c, 2, held1.at[c, :, 1 - bit[b]], got2.at[c], peers[b])
 
     def stage3(c):
@@ -515,32 +506,26 @@
         own_half(c).wait()
         stage0(c).wait_recv()
         held[c] = held[c] + got0[c]
-        either(c, lambda odd: stage1(c, odd).start())
+        stage1(c).start()
 
     def after1(c):
-        def act(odd):
-            stage1(c, odd).wait_recv()
-            kept = held[c, :, bit[2]] if odd else held[c, :, :, bit[1]]
-            held1[c] = kept + got1[c]
-            stage2(c, odd).start()
-
-        either(c, act)
+        stage1(c).wait_recv()
+        kept = held[c, :, bit[2]] if c % 2 else held[c, :, :, bit[1]]
+        held1[c] = kept + got1[c]
+        stage2(c).start()
 
     def after2(c):
-        def act(odd):
-            stage2(c, odd).wait_recv()
-            held2[c] = held1[c, :, bit[1 if odd else 2]] + got2[c]
-
-        either(c, act)
+        stage2(c).wait_recv()
+        held2[c] = held1[c, :, bit[1 if c % 2 else 2]] + got2[c]
         stage3(c).start()
 
     def after3(c):
         stage3(c).wait_recv()
-        done[:, columns_of(c, count - 1)] = held2[c, bit[3]] + got3[c]
+        done[:, columns_of(c, 0)] = held2[c, bit[3]] + got3[c]
 
     def settle():
         for c in range(count):
-            for copy in (stage0(c), stage1(c, c % 2), stage2(c, c % 2), stage3(c)):
+            for copy in (stage0(c), stage1(c), stage2(c), stage3(c)):
                 copy.wait_send()
 
     return begin, after0, after1, after2, after3, settle
@@ -599,12 +584,14 @@
 
     if fused:
         *early_refs, done_s, other_a, early_sems = refs[10:]
-        begin, after0, after1, after2, after3, settle = reducer(packed, device, side, IN_FIRST, CHUNKS - 1, early_refs, done_s)
-        span_e = packed.shape[-1] // CHUNKS
+        begin, after0, after1, after2, after3, settle = reducer(
+            packed, device, side, packed.shape[-1] - EARLY * FIRST_CUT, early_refs, done_s
+        )
+        half_e = packed.shape[-1] // 2
+        tail_e = EARLY * FIRST_CUT - half_e
         peers = [{"dp": bit_peer(device, b), "tensor": side} for b in range(4)]
-        sent_e = (IN_FIRST - 1) * span_e
         swap = pltpu.make_async_remote_copy(
-            src_ref=done_s.at[:, pl.ds(span_e, sent_e)],
+            src_ref=done_s.at[:, pl.ds(tail_e, half_e)],
             dst_ref=other_a,
             send_sem=early_sems.at[0],
             recv_sem=early_sems.at[1],
@@ -622,11 +609,11 @@
             copy.wait()
 
     if fused:
-        for late, act in ((0, begin), (1, after0), (3, after1), (5, after2), (6, after3)):
-            since = tick - late
-            @pl.when((since >= 0) & (since % 2 == 0) & (since // 2 < IN_FIRST))
-            def _():
-                act(since // 2)
+        for c in range(EARLY):
+            for at, act in ((0, begin), (1 + c, after0), (5 + c, after1), (8 + c, after2), (12, after3)):
+                @pl.when(tick == at)
+                def _():
+                    act(c)
 
         @pl.when(tick == 12)
         def _():
@@ -742,7 +729,7 @@
             sums[i][:, part] = (grad_s[i, 0, 0, :, part].astype(F32) + near_s[i, 0, :, part].astype(F32)).astype(BF)
         if fused:
             swap.wait_recv()
-            done_out[...] = done_s[:, pl.ds(0, span_e)]
+            done_out[...] = done_s[:, pl.ds(0, tail_e)]
             other_out[...] = other_a[...]
             settle()
             swap.wait_send()
@@ -769,12 +756,12 @@
     fused = packed is not None
     more_in, more_out, more_scratch = [], [], []
     if fused:
-        block, cut = packed.shape[-2], packed.shape[-1] // CHUNKS
+        block, half_e = packed.shape[-2], packed.shape[-1] // 2
         more_in = [packed]
-        more_out = [shape((block, cut), BF), shape((block, (IN_FIRST - 1) * cut), BF)]
-        more_scratch = reducer_scratch(IN_FIRST, block, cut) + [
-            pltpu.VMEM((block, IN_FIRST * cut), BF),
-            pltpu.VMEM((block, (IN_FIRST - 1) * cut), BF),
+        more_out = [shape((block, EARLY * FIRST_CUT - half_e), BF), shape((block, half_e), BF)]
+        more_scratch = reducer_scratch(EARLY, block, FIRST_CUT) + [
+            pltpu.VMEM((block, EARLY * FIRST_CUT), BF),
+            pltpu.VMEM((block, half_e), BF),
             pltpu.SemaphoreType.DMA((2,)),
         ]
     return pl.pallas_call(
@@ -1161,7 +1148,7 @@
     bits, hid, vec_all, dq, dk, dv, wq, wk, wv, gmix, ext, sum_k, sum_v, relay, first_done, first_other, packed,
     gin, late_out, vec_out, early_out,
     loc_s, far_s, unit_s, mine_s, norm_s, send_c, recv_c, send_p, recv_p, give_c, give_p, late_s, small_s,
-    vec_s, vec_r, done_s, other_b, sems_a, sems_b, loc_sems, *stage_refs,
+    vec_s, vec_r, done_s, sems_a, sems_b, loc_sems, *stage_refs,
 ):
     device = lax.axis_index("dp")
     side = lax.axis_index("tensor")
@@ -1191,14 +1178,10 @@
 
     share = remote(relay, far_s, peers[1])
 
-    in_last = CHUNKS - IN_FIRST
-    begin, after0, after1, after2, after3, settle = reducer(packed, device, side, in_last, in_last - 1, stage_refs[-10:], done_s)
-    cut = packed.shape[-1] // CHUNKS
-    half_cut = cut // 2
-    swap_e = remote(first_done.at[:, pl.ds(half_cut, half_cut)], other_b, across)
+    begin, after0, after1, after2, after3, settle = reducer(packed, device, side, 0, stage_refs[-10:], done_s)
 
     def each(act):
-        for c in range(in_last):
+        for c in range(EARLY):
             act(c)
 
     each(begin)
@@ -1328,20 +1311,18 @@
     late_out[...] = source[0, 0, :, pl.ds(0, 3 * width)].astype(F32)
     vec_s[...] = source[0, 0, :, pl.ds(3 * width, 128)]
     swap = remote(vec_s, vec_r, across)
-    swap_e.wait_recv()
-    last_e = in_last * cut
-    early_out[:, pl.ds(0, half_cut)] = done_s[:, pl.ds(0, half_cut)].astype(F32) + other_b[...].astype(F32)
-    early_out[:, pl.ds(half_cut, last_e - half_cut)] = done_s[:, pl.ds(half_cut, last_e - half_cut)].astype(
-        F32
-    ) + first_other[:, pl.ds(0, last_e - half_cut)].astype(F32)
-    early_out[:, pl.ds(last_e, half_cut)] = first_done[:, pl.ds(0, half_cut)].astype(F32) + first_other[
-        :, pl.ds(last_e - half_cut, half_cut)
-    ].astype(F32)
+    last_e = done_s.shape[1]
+    early_out[:, pl.ds(0, last_e)] = done_s[...].astype(F32) + first_other[:, pl.ds(0, last_e)].astype(F32)
+    rest_e = first_done.shape[1]
+    early_out[:, pl.ds(last_e, rest_e)] = first_done[...].astype(F32) + first_other[:, pl.ds(last_e, rest_e)].astype(F32)
     settle()
     swap.wait_recv()
-    vec_out[0] = vec_s[...].astype(F32)
-    vec_out[1] = vec_r[...].astype(F32)
-    for copy in stages + [share, swap_e, y_cont, y_prompt, swap]:
+    own_v, got_v = vec_s[...].astype(F32), vec_r[...].astype(F32)
+    vec_out[0:8, :] = own_v[0:8] + got_v[8:16]
+    vec_out[8:16, :] = own_v[16:24] + got_v[24:32]
+    vec_out[16:24, :] = own_v[32:40] + got_v[32:40]
+    vec_out[24:32, :] = own_v[40:48] + jnp.where(row_id < 2, 0.0, got_v[40:48])
+    for copy in stages + [share, y_cont, y_prompt, swap]:
         copy.wait_send()
     for copy in (back_c, back_p):
         copy.wait_recv()
@@ -1361,8 +1342,8 @@
     vmem = pl.BlockSpec(memory_space=pltpu.VMEM)
     hbm = pl.BlockSpec(memory_space=pl.ANY)
     shape = jax.ShapeDtypeStruct
-    copies = 7 + bits
-    cut = packed.shape[-1] // CHUNKS
+    copies = 6 + bits
+    cut = (packed.shape[-1] - EARLY * FIRST_CUT) // EARLY
     stages = []
     for bit in range(bits):
         left = ranks >> (bit + 1)
@@ -1372,7 +1353,7 @@
         functools.partial(final_kernel, bits),
         in_specs=[vmem] * 15 + [hbm],
         out_specs=[hbm, vmem, vmem, vmem],
-        out_shape=[shape((rows, D), BF), shape((block, 3 * width), F32), shape((2, block, 128), F32), shape((block, packed.shape[-1] // 2), F32)],
+        out_shape=[shape((rows, D), BF), shape((block, 3 * width), F32), shape((32, 128), F32), shape((block, packed.shape[-1] // 2), F32)],
         scratch_shapes=[
             pltpu.VMEM((2, prompt, width), BF),
             pltpu.VMEM((2, prompt, 128), BF),
@@ -1389,14 +1370,13 @@
             pltpu.VMEM((8, D + 128), F32),
             pltpu.VMEM((block, 128), BF),
             pltpu.VMEM((block, 128), BF),
-            pltpu.VMEM((block, (CHUNKS - IN_FIRST) * cut), BF),
-            pltpu.VMEM((block, cut // 2), BF),
+            pltpu.VMEM((block, EARLY * cut), BF),
             pltpu.SemaphoreType.DMA((copies,)),
             pltpu.SemaphoreType.DMA((copies,)),
             pltpu.SemaphoreType.DMA((2,)),
         ]
         + stages
-        + reducer_scratch(CHUNKS - IN_FIRST, block, cut),
+        + reducer_scratch(EARLY, block, cut),
         compiler_params=pltpu.CompilerParams(vmem_limit_bytes=56 << 20, collective_id=1, has_side_effects=True),
         cost_estimate=pl.CostEstimate(flops=5 * 10**9, bytes_accessed=20 * 10**6, transcendentals=0),
         name="finish",
@@ -1457,12 +1437,12 @@
 
 def side_by_side(parts):
     total = sum(part.shape[0] for part in parts)
-    row, at = jnp.zeros((1, total), F32), 0
+    row, at = jnp.zeros((total,), F32), 0
     for part in parts:
         size = part.shape[0]
-        row = row + jnp.pad(part.astype(F32)[None], ((0, 0), (at, total - at - size)))
+        row = row + jnp.pad(part.astype(F32), (at, total - at - size))
         at += size
-    return row
+    return row[None]
 
 
 def half_of(value, which):
@@ -1557,8 +1537,8 @@
     ) = attend(
         prompt_start,
         cont_gap,
-        seg_len,
-        dilation_rate,
+        seg_len.T,
+        dilation_rate.T,
         hidden_in,
         vectors,
         query_weight,
@@ -1623,13 +1603,11 @@
             *early,
             packed.reshape(2, 2, 2, 2, D // ranks, -1),
         )
-        ffn_gain_grad, ffn_bias_grad, inner_bias_grad = [vec[0, i, :per_u] + vec[1, 8 + i, :per_u] for i in range(3)]
-        sub_gain_grad, sub_bias_grad = [vec[0, 16 + i, :per_w] + vec[1, 24 + i, :per_w] for i in range(2)]
-        out_bias_grad, mid_gain_grad, mid_bias_grad, outer_bias_grad = [
-            vec[0, 32 + i, :per_d] + vec[1, 32 + i, :per_d] for i in range(4)
-        ]
-        query_bias_grad, value_bias_grad = [vec[0, 40 + i, :per_w] for i in range(2)]
-        pre_gain_grad, pre_bias_grad = [vec[0, 42 + i, :per_d] + vec[1, 42 + i, :per_d] for i in range(2)]
+        ffn_gain_grad, ffn_bias_grad, inner_bias_grad = [vec[i, :per_u] for i in range(3)]
+        sub_gain_grad, sub_bias_grad = [vec[8 + i, :per_w] for i in range(2)]
+        out_bias_grad, mid_gain_grad, mid_bias_grad, outer_bias_grad = [vec[16 + i, :per_d] for i in range(4)]
+        query_bias_grad, value_bias_grad = [vec[24 + i, :per_w] for i in range(2)]
+        pre_gain_grad, pre_bias_grad = [vec[26 + i, :per_d] for i in range(2)]
     else:
         pre_normed, pre_unit, pre_scale = norm_rows(hidden_in.astype(F32), pre_gain_f, pre_bias.astype(F32))
         pre_low = pre_normed.astype(BF)

time: 327 us -> 302 us (0.924)
  Pallas kernels: 298 us -> 284 us
  local copies, waits for them, and re-layouts: 17.6 us -> 10.6 us
  other arithmetic: 6.19 us -> 2.38 us
    pallas_call x1, Pallas kernels: 107 us -> 92.5 us  [attend_back(): pl.pallas_call(functools.partial(bwd_kernel, fused), grid=(pairs, rows //...]
    broadcast_in_dim x13 -> x1, local copies, waits for them, and re-layouts: 8.91 us -> 0.65 us  [side_by_side(): return row[None]]
    squeeze x0 -> x3, local copies, waits for them, and re-layouts: none -> 3.96 us  [the longest x1 1.37 us: body(): vec[16 + i, :per_d]]
    add x4 -> x1, other arithmetic: 4.65 us -> 0.85 us  [side_by_side(): row = row + jnp.pad(part.astype(F32), (at, total - at - size))]
where the time goes in v1:
time: 302 us; the launch traced here: 298 us
  Pallas kernels  284 us (94%)
  local copies, waits for them, and re-layouts  10.6 us (4%)
    pallas_call x1, Pallas kernels, attend_back(): pl.pallas_call(functools.partial(bwd_kernel, fused), grid=(pairs, rows //...  92.5 us
    pallas_call x1, Pallas kernels, finish(): pl.pallas_call(functools.partial(final_kernel, bits), in_specs=[vmem] * 1...  66.3 us
    pallas_call x1, Pallas kernels, attend(): pl.pallas_call(fwd_kernel, grid_spec=pltpu.PrefetchScalarGridSpec(num_sca...  63.4 us
    pallas_call x1, Pallas kernels, middle(): pl.pallas_call(mid_kernel, in_specs=[vmem] * 4 + [hbm] * 9, out_specs=[vm...  61.6 us

profile of v1, /device:TPU:0, one launch (start us, length us, event | category | flops | bytes accessed | tf_op | source)
XLA Modules:
  0.0 297.7 jit_solution(3104239971523562128)
XLA Ops:
  0.7 0.9 convert_add_fusion
  1.5 0.6 broadcast_in_dim.3.vec.vec_hbm.vec_all
  2.2 63.4 %attend.1 = (bf16[6,1280,2304]{2,1,0:T(8,128)(2,1)}, f32[1280,384]{1,0:T(8,128)}, bf16[1280,384]{1,0:T(8,128)(2,1)}, bf16[768,384]{1,0:T(8,128)(2,1)}, bf16[768,...) custom-call(s32[4]{0:T(128)} %starts.1, ...), custom_call_target="tpu_custom_call" | custom-call | flops 20000000000 | bytes 60000000 | tf_op jit(solution)/shard_map/attend/pallas_call | solution.py:395
  65.6 61.6 %middle.1 = (bf16[640,768]{1,0:T(8,128)(2,1)}, bf16[640,384]{1,0:T(8,128)(2,1)}, bf16[640,384]{1,0:T(8,128)(2,1)}, bf16[640,768]{1,0:T(8,128)(2,1)}, bf16[768,69...) custom-call(bf16[640,384]{1,0:T(8,128)(2,1)} %get-tuple-element.55.a, ...), custom_call_target="tpu_custom_call" | custom-call | flops 20999999488 | bytes 30000000 | tf_op jit(solution)/shard_map/middle/pallas_call | solution.py:1101
  127.2 92.5 %attend_back.1 = (bf16[1280,384]{1,0:T(8,128)(2,1)}, bf16[1280,384]{1,0:T(8,128)(2,1)}, bf16[1280,384]{1,0:T(8,128)(2,1)}, bf16[512,384]{1,0:T(8,128)(2,1)}, bf1...) custom-call(bf16[1280,384]{1,0:T(8,128)(2,1)} %get-tuple-element.63., ...), custom_call_target="tpu_custom_call" | custom-call | flops 30000001024 | bytes 60000000 | tf_op jit(solution)/shard_map/attend_back/pallas_call | solution.py:767
  219.8 0.0 copy-start.2
  219.8 66.3 %finish.1 = (bf16[1280,768]{1,0:T(8,128)(2,1)}, f32[48,1152]{1,0:T(8,128)}, f32[32,128]{1,0:T(8,128)}, f32[48,3456]{1,0:T(8,128)}) custom-call(bf16[1280,768]{1,0:T(8,128)(2,1)} %hid.3, f32[1,10752]{1,0:T(1,128)} %broadcast_in_dim.3.vec.vec_hbm.vec_all, bf16[1280,384]{1,0:T(8,128)(2,1)} %get-tuple-element.75.dq, bf16[1280,384]{1,0:T(8,128)(2,1)} %get-tuple-element.76.dk, ...), custom_call_target="tpu_custom_call" | custom-call | flops 5000000000 | bytes 20000000 | tf_op jit(solution)/shard_map/finish/pallas_call | solution.py:1352
  286.0 0.0 copy-start.1
  286.0 1.8 fusion
  287.8 1.9 slice_bitcast_fusion
  289.7 1.4 slice_bitcast_fusion.2
  291.1 1.3 slice_bitcast_fusion.9
  292.4 1.3 slice_bitcast_fusion.3
  293.7 0.0 copy-done.2
  293.7 0.0 copy-done.1
  293.7 0.1 broadcast_select_fusion.1
  294.0 0.0 copy-start
  294.0 1.4 pad_maximum_fusion
  295.4 0.8 copy-done
  296.3 1.3 copy.47
  (4 shorter events, 0.1 us)
Async XLA Ops:
  219.8 73.9 %copy-start.2 = (bf16[640,768]{1,0:T(8,128)(2,1)S(1)}, bf16[640,768]{1,0:T(8,128)(2,1)}, u32[]{:S(2)}) copy-start(bf16[640,768]{1,0:T(8,128)(2,1)} %get-tuple-element.74) | copy-start | bytes 2949124
  286.0 7.7 %copy-start.1 = (bf16[640,768]{1,0:T(8,128)(2,1)S(1)}, bf16[640,768]{1,0:T(8,128)(2,1)}, u32[]{:S(2)}) copy-start(bf16[640,768]{1,0:T(8,128)(2,1)} %get-tuple-element.62.out_half) | copy-start | bytes 2949124
  294.0 2.3 copy-start

commit v2 on v1

--- a/solution.py
+++ b/solution.py
@@ -32,6 +32,57 @@
 
 def low_half(rows):
     return lax.broadcasted_iota(jnp.int32, (rows, 128), 1) < HD
+
+
+MASKED = -1e30
+CLASSES = 36
+
+
+def lane_classes(head):
+    lane = lax.broadcasted_iota(jnp.int32, (8, 128), 1) - (HD if head == 0 else 0)
+    number = lane.astype(F32)
+    main = lane < CLASSES
+    number = jnp.where(main, number, 4.0 * (number - CLASSES) + 3.0)
+    number = jnp.where((lane >= 0) & (lane < CLASSES + CLASSES // 4), number, -5.0)
+    combo = jnp.floor((number + 0.5) * 0.25)
+    step0 = jnp.floor((combo + 0.5) * (1.0 / 3.0))
+    step1 = combo - 3.0 * step0
+    rest = number - 4.0 * combo
+    flag1 = jnp.where(rest > 1.5, 1.0, 0.0)
+    return number, step0, step1, flag1, rest - 2.0 * flag1, jnp.where(main, 0.0, 1.0)
+
+
+def key_side(keys, first, cells, classes):
+    size = keys.shape[0]
+    at = first + lax.broadcasted_iota(jnp.int32, (8, size), 1).astype(F32)
+    base = jnp.full((8, size), 0.0, F32) + first
+    row = lax.broadcasted_iota(jnp.int32, (8, size), 0)
+
+    def cell(i):
+        return cells[i][:, 0:1]
+
+    step0 = jnp.floor((at + 0.5) * cell(0)) - jnp.floor((base + 0.5) * cell(0))
+    step1 = jnp.floor((at + 0.5) * cell(1)) - jnp.floor((base + 0.5) * cell(1))
+    rest1 = at - cell(2) * jnp.floor((at + 0.5) * cell(3))
+    rest2 = at - cell(4) * jnp.floor((at + 0.5) * cell(5))
+    flag1 = jnp.where(rest1 == jnp.where(row == 0, cell(6), cell(7)), 2.0, 0.0)
+    flag2 = jnp.where(rest2 == jnp.where(row == 0, cell(8), cell(9)), 1.0, 0.0)
+    columns = jnp.transpose(4.0 * (3.0 * step0 + step1) + flag1 + flag2)
+    low = low_half(size)
+    hot = [jnp.where(columns[:, h : h + 1] == classes[h][0][0:1], 1.0, 0.0).astype(BF) for h in range(2)]
+    return [jnp.where(low, keys, hot[0]), jnp.where(low, hot[1], keys)]
+
+
+def query_side(head, queries, qc, first, cells, lanes, low):
+    _, step0, step1, flag1, flag2, small = lanes
+    base = jnp.zeros((8, 128), F32) + first
+    kc0 = (jnp.floor((base + 0.5) * cells[0]) + step0)[0:1]
+    kc1 = jnp.where(flag1 > 0.5, jnp.floor((base + 0.5) * cells[1]) + step1, -1.0)[0:1]
+    weight = jnp.where(qc[0] == kc0, 1.0, 0.0) + jnp.where(qc[1 + head] == kc1, 1.0, 0.0)
+    weight = weight + qc[3 + head] * flag2[0:1]
+    logs = jnp.maximum(jnp.log2(weight), MASKED)
+    logs = jnp.where(small[0:1] > 0.5, logs - logs.astype(BF).astype(F32), logs).astype(BF)
+    return jnp.where(low, queries, logs) if head == 0 else jnp.where(low, logs, queries)
 
 
 def settings(seg, rate, pair):
@@ -91,7 +142,7 @@
     starts, gaps, seg, rate, hid, vec, wq, wk, wv, w1, wo, vec_hbm,
     e_ref, li_ref, q_out, k_out, v_out, kp_out, vp_out, o_out, mine_out, got_out,
     w1_got, w1_swap, wo_got, wo_swap, vec_got,
-    t_s, kc_s, kv_s, low_s, q_s, ko_s, vo_s, o_s, sems_a, sems_b, loc_sems,
+    t_s, ka_s, kv_s, low_s, q_s, qe_s, ko_s, vo_s, o_s, sems_a, sems_b, loc_sems,
 ):
     pair = pl.program_id(0)
     step = pl.program_id(1)
@@ -206,7 +257,9 @@
         for p in range(1, n_pairs):
             to_far(p).start()
         for at in range(0, rows, TILE):
-            q_s[at : at + TILE, :] = ((dot_nn(low_s[at : at + TILE, :], wq[...]) + query_bias) * 0.125).astype(BF)
+            scaled = (dot_nn(low_s[at : at + TILE, :], wq[...]) + query_bias) * 0.125
+            q_s[at : at + TILE, :] = scaled.astype(BF)
+            qe_s[at : at + TILE, :] = (scaled * LOG2E).astype(BF)
         to_far(0).wait_recv()
         relay(0).start()
 
@@ -224,9 +277,7 @@
 
     lanes = pl.ds(pl.multiple_of(pair * 128, 128), 128)
     low = low_half(TILE)
-    q = q_s[pl.ds(pl.multiple_of(step * TILE, TILE), TILE), lanes]
-    zero = jnp.zeros_like(q)
-    qs = [jnp.where(low, q, zero), jnp.where(low, zero, q)]
+    q = qe_s[pl.ds(pl.multiple_of(step * TILE, TILE), TILE), lanes]
     row = lax.broadcasted_iota(jnp.int32, (TILE, 128), 0).astype(F32)
     group = device // GDEV
     start = starts[group]
@@ -236,104 +287,109 @@
     cells = settings(seg, rate, side * n_pairs + pair)
     at_q = base_q.astype(F32) + row
     qc = codes(at_q, cells, -2.0)
+    classes = [lane_classes(h) for h in range(2)]
+    first_at = start.astype(F32)
 
     @pl.when(step == 0)
     def _():
-        ahead = lax.broadcasted_iota(jnp.int32, (8, 128), 1).astype(F32) + start.astype(F32)
-        for j in range(PROMPT // 128):
-            for i, c in enumerate(codes(ahead + j * 128.0, cells, -1.0)):
-                kc_s[i, :, j * 128 : (j + 1) * 128] = c
-
-    def logits(mx, keys, kc, causal, at, span):
-        out = []
-        for h in range(2):
-            s = dot_nt(qs[h], keys)
-            top = mx[h]
-            for g in range(span // 128):
-                part = slice(g * 128, (g + 1) * 128)
-                w = jnp.where(qc[0] == kc[0][:, part], 1.0, 0.0)
-                w = w + jnp.where(qc[1 + h] == kc[1 + h][:, part], 1.0, 0.0)
-                w = w + qc[3 + h] * kc[3 + h][:, part]
-                if causal is not None:
-                    w = jnp.where(causal[:, part], w, 0.0)
-                t = s[:, part] * LOG2E + jnp.log2(w)
-                t_s[h, :, pl.ds(at + g * 128, 128)] = t
-                top = jnp.maximum(top, t)
-            out.append(top)
-        return tuple(out)
-
-    def weigh(carry, vals, m, at, span):
-        sums, accs = carry
-        ns, na = [], []
-        for h in range(2):
-            total = sums[h]
-            parts = []
-            for g in range(span // 128):
-                e = jnp.exp2(t_s[h, :, pl.ds(at + g * 128, 128)] - m[h])
-                total = total + e
-                parts.append(e.astype(BF))
-            el = jnp.concatenate(parts, axis=1)
-            e_ref[h, :, pl.ds(at, span)] = el
-            ns.append(total)
-            na.append(accs[h] + dot_nn(el, vals))
-        return (tuple(ns), tuple(na))
+        for j in range(GDEV):
+            first = first_at + (xor_bits(j, member) * CHUNK).astype(F32)
+            for h, made in enumerate(key_side(kv_s[j, 0, :, lanes], first, cells, classes)):
+                ka_s[h, j * CHUNK : (j + 1) * CHUNK, :] = made
+
+    def logits(h, top, keys, first, causal, at, width):
+        t = dot_nt(query_side(h, q, qc, first, cells, classes[h], low), keys)
+        if causal is not None:
+            t = jnp.where(causal, t, MASKED)
+        t_s[h, :, pl.ds(at, width)] = t
+        for g in range(width // 128):
+            top = jnp.maximum(top, t[:, g * 128 : (g + 1) * 128])
+        return top
+
+    def weigh(h, carry, vals, m, at, width):
+        total, acc = carry
+        parts = []
+        for g in range(width // 128):
+            e = jnp.exp2(t_s[h, :, pl.ds(at + g * 128, 128)] - m)
+            total = total + e
+            parts.append(e.astype(BF))
+        el = jnp.concatenate(parts, axis=1)
+        e_ref[h, :, pl.ds(at, width)] = el
+        return total, acc + dot_nn(el, vals)
 
     def finish_rows(carry):
-        sums, accs = carry
+        (sums0, acc0), (sums1, acc1) = carry
+        sums, accs = (sums0, sums1), (acc0, acc1)
         li = [1.0 / jnp.sum(s, axis=1, keepdims=True) for s in sums]
         lfull = jnp.where(low, li[0], li[1])
         li_ref[...] = lfull
         o_s[pl.ds(pl.multiple_of(step * TILE, TILE), TILE), lanes] = (jnp.where(low, accs[0], accs[1]) * lfull).astype(BF)
 
     def tops(mx):
-        return [jnp.broadcast_to(jnp.max(x, axis=1, keepdims=True), (TILE, 128)) for x in mx]
+        return jnp.broadcast_to(jnp.max(mx, axis=1, keepdims=True), (TILE, 128))
 
     neg = jnp.full((TILE, 128), -jnp.inf, F32)
     zf = jnp.zeros((TILE, 128), F32)
 
-    def key_codes(at, span):
-        return [kc_s[i, 0:1, pl.ds(at, span)] for i in range(5)]
+    def held_keys(h, at):
+        return ka_s[h, pl.ds(at, CHUNK), :]
 
     @pl.when(step < PTILES)
     def _():
-        def one(j, mx):
-            at = pl.multiple_of(j * CHUNK, CHUNK)
-            held = xor_bits(j, member)
-            return logits(
-                mx, kv_s[held, 0, :, lanes], key_codes(at, CHUNK), None, pl.multiple_of(held * CHUNK, CHUNK), CHUNK
-            )
-
-        mx = lax.fori_loop(0, member, one, (neg, neg))
-        at = pl.multiple_of(member * CHUNK, CHUNK)
         rows_id = lax.broadcasted_iota(jnp.int32, (TILE, CHUNK), 0) + step * TILE
         cols = lax.broadcasted_iota(jnp.int32, (TILE, CHUNK), 1)
-        mx = logits(mx, kv_s[0, 0, :, lanes], key_codes(at, CHUNK), cols <= rows_id, 0, CHUNK)
-        m = tops(mx)
-
-        def two(j, carry):
-            held = xor_bits(j, member)
-            return weigh(carry, kv_s[held, 1, :, lanes], m, pl.multiple_of(held * CHUNK, CHUNK), CHUNK)
-
-        finish_rows(lax.fori_loop(0, member + 1, two, ((zf, zf), (zf, zf))))
+        here = first_at + (member * CHUNK).astype(F32)
+
+        def place(j):
+            return pl.multiple_of(xor_bits(j, member) * CHUNK, CHUNK)
+
+        def score(h, j, top):
+            return logits(h, top, held_keys(h, place(j)), first_at + (j * CHUNK).astype(F32), None, place(j), CHUNK)
+
+        def spread(h, j, m, carry):
+            return weigh(h, carry, kv_s[xor_bits(j, member), 1, :, lanes], m, place(j), CHUNK)
+
+        top = lax.fori_loop(0, member, lambda j, top: score(0, j, top), neg)
+        m0 = tops(logits(0, top, held_keys(0, 0), here, cols <= rows_id, 0, CHUNK))
+
+        def both(j, carry):
+            return spread(0, j, m0, carry[0]), score(1, j, carry[1])
+
+        first, top = lax.fori_loop(0, member, both, ((zf, zf), neg))
+        first = weigh(0, first, kv_s[0, 1, :, lanes], m0, 0, CHUNK)
+        m1 = tops(logits(1, top, held_keys(1, 0), here, cols <= rows_id, 0, CHUNK))
+        finish_rows((first, lax.fori_loop(0, member + 1, lambda j, carry: spread(1, j, m1, carry), (zf, zf))))
 
     @pl.when(step >= PTILES)
     def _():
-        own = pl.ds(pl.multiple_of((step - PTILES) * TILE, TILE), TILE)
-        mx = (neg, neg)
-        for j in range(GDEV):
-            at = pl.multiple_of(xor_bits(j, member) * CHUNK, CHUNK)
-            mx = logits(mx, kv_s[j, 0, :, lanes], key_codes(at, CHUNK), None, j * CHUNK, CHUNK)
+        own_rows = pl.ds(pl.multiple_of((step - PTILES) * TILE, TILE), TILE)
         rows_id = lax.broadcasted_iota(jnp.int32, (TILE, CONT), 0)
         cols = lax.broadcasted_iota(jnp.int32, (TILE, CONT), 1)
-        ahead = lax.broadcasted_iota(jnp.int32, (8, 128), 1).astype(F32) + base_q.astype(F32)
-        parts = [codes(ahead + j * 128.0, cells, -1.0) for j in range(CONT // 128)]
-        own_codes = [jnp.concatenate([part[i] for part in parts], axis=1)[0:1] for i in range(5)]
-        mx = logits(mx, ko_s[own, lanes], own_codes, cols <= rows_id, PROMPT, CONT)
-        m = tops(mx)
-        carry = ((zf, zf), (zf, zf))
-        for j in range(GDEV):
-            carry = weigh(carry, kv_s[j, 1, :, lanes], m, j * CHUNK, CHUNK)
-        finish_rows(weigh(carry, vo_s[own, lanes], m, PROMPT, CONT))
+        own_at = base_q.astype(F32)
+        own = key_side(ko_s[own_rows, lanes], own_at, cells, classes)
+
+        def score(h, j, top):
+            if j == GDEV:
+                return logits(h, top, own[h], own_at, cols <= rows_id, PROMPT, CONT)
+            first = first_at + (xor_bits(j, member) * CHUNK).astype(F32)
+            return logits(h, top, held_keys(h, j * CHUNK), first, None, j * CHUNK, CHUNK)
+
+        def spread(h, j, m, carry):
+            if j == GDEV:
+                return weigh(h, carry, vo_s[own_rows, lanes], m, PROMPT, CONT)
+            return weigh(h, carry, kv_s[j, 1, :, lanes], m, j * CHUNK, CHUNK)
+
+        top = neg
+        for j in range(GDEV + 1):
+            top = score(0, j, top)
+        m0, top, first, second = tops(top), neg, (zf, zf), (zf, zf)
+        for j in range(GDEV + 1):
+            first = spread(0, j, m0, first)
+            top = score(1, j, top)
+        m1 = tops(top)
+        for j in range(GDEV + 1):
+            second = spread(1, j, m1, second)
+        finish_rows((first, second))
 
     end = pl.num_programs(1) - 1
     for p in range(n_pairs):
@@ -405,9 +461,10 @@
             + [hbm] * 13,
             scratch_shapes=[
                 pltpu.VMEM((2, TILE, span), F32),
-                pltpu.VMEM((5, 8, PROMPT), F32),
+                pltpu.VMEM((2, PROMPT, 128), BF),
                 pltpu.VMEM((GDEV, 2, CHUNK, width), BF),
                 pltpu.VMEM((rows, D), BF),
+                pltpu.VMEM((rows, width), BF),
                 pltpu.VMEM((rows, width), BF),
                 pltpu.VMEM((conts, width), BF),
                 pltpu.VMEM((conts, width), BF),

time: 302 us -> 297 us (0.983)
  Pallas kernels: 284 us -> 279 us
where the time goes in v2:
time: 297 us; the launch traced here: 293 us
  Pallas kernels  279 us (94%)
  local copies, waits for them, and re-layouts  10.6 us (4%)
    pallas_call x1, Pallas kernels, attend_back(): pl.pallas_call(functools.partial(bwd_kernel, fused), grid=(pairs, rows //...  92.2 us
    pallas_call x1, Pallas kernels, finish(): pl.pallas_call(functools.partial(final_kernel, bits), in_specs=[vmem] * 1...  66.4 us
    pallas_call x1, Pallas kernels, attend(): pl.pallas_call(fwd_kernel, grid_spec=pltpu.PrefetchScalarGridSpec(num_sca...  61.3 us
    pallas_call x1, Pallas kernels, middle(): pl.pallas_call(mid_kernel, in_specs=[vmem] * 4 + [hbm] * 9, out_specs=[vm...  59.2 us

profile of v2, /device:TPU:0, one launch (start us, length us, event | category | flops | bytes accessed | tf_op | source)
XLA Modules:
  0.0 293.1 jit_solution(16106490868689367788)
XLA Ops:
  0.7 0.9 convert_add_fusion
  1.5 0.6 broadcast_in_dim.3.vec.vec_hbm.vec_all
  2.2 61.3 %attend.1 = (bf16[6,1280,2304]{2,1,0:T(8,128)(2,1)}, f32[1280,384]{1,0:T(8,128)}, bf16[1280,384]{1,0:T(8,128)(2,1)}, bf16[768,384]{1,0:T(8,128)(2,1)}, bf16[768,...) custom-call(s32[4]{0:T(128)} %starts.1, ...), custom_call_target="tpu_custom_call" | custom-call | flops 20000000000 | bytes 60000000 | tf_op jit(solution)/shard_map/attend/pallas_call | solution.py:451
  63.4 59.2 %middle.1 = (bf16[640,768]{1,0:T(8,128)(2,1)}, bf16[640,384]{1,0:T(8,128)(2,1)}, bf16[640,384]{1,0:T(8,128)(2,1)}, bf16[640,768]{1,0:T(8,128)(2,1)}, bf16[768,69...) custom-call(bf16[640,384]{1,0:T(8,128)(2,1)} %get-tuple-element.55.a, ...), custom_call_target="tpu_custom_call" | custom-call | flops 20999999488 | bytes 30000000 | tf_op jit(solution)/shard_map/middle/pallas_call | solution.py:1158
  122.7 92.2 %attend_back.1 = (bf16[1280,384]{1,0:T(8,128)(2,1)}, bf16[1280,384]{1,0:T(8,128)(2,1)}, bf16[1280,384]{1,0:T(8,128)(2,1)}, bf16[512,384]{1,0:T(8,128)(2,1)}, bf1...) custom-call(bf16[1280,384]{1,0:T(8,128)(2,1)} %get-tuple-element.63., ...), custom_call_target="tpu_custom_call" | custom-call | flops 30000001024 | bytes 60000000 | tf_op jit(solution)/shard_map/attend_back/pallas_call | solution.py:824
  214.9 0.0 copy-start.2
  214.9 66.4 %finish.1 = (bf16[1280,768]{1,0:T(8,128)(2,1)}, f32[48,1152]{1,0:T(8,128)}, f32[32,128]{1,0:T(8,128)}, f32[48,3456]{1,0:T(8,128)}) custom-call(bf16[1280,768]{1,0:T(8,128)(2,1)} %hid.3, f32[1,10752]{1,0:T(1,128)} %broadcast_in_dim.3.vec.vec_hbm.vec_all, bf16[1280,384]{1,0:T(8,128)(2,1)} %get-tuple-element.75.dq, bf16[1280,384]{1,0:T(8,128)(2,1)} %get-tuple-element.76.dk, ...), custom_call_target="tpu_custom_call" | custom-call | flops 5000000000 | bytes 20000000 | tf_op jit(solution)/shard_map/finish/pallas_call | solution.py:1409
  281.4 0.0 copy-start.1
  281.4 1.8 fusion
  283.2 1.9 slice_bitcast_fusion
  285.1 1.4 slice_bitcast_fusion.2
  286.4 1.3 slice_bitcast_fusion.9
  287.7 1.3 slice_bitcast_fusion.3
  289.0 0.0 copy-done.2
  289.0 0.0 copy-done.1
  289.0 0.1 broadcast_select_fusion.1
  289.3 0.0 copy-start
  289.4 1.4 pad_maximum_fusion
  290.8 0.8 copy-done
  291.6 1.3 copy.47
  (4 shorter events, 0.1 us)
Async XLA Ops:
  214.9 74.1 %copy-start.2 = (bf16[640,768]{1,0:T(8,128)(2,1)S(1)}, bf16[640,768]{1,0:T(8,128)(2,1)}, u32[]{:S(2)}) copy-start(bf16[640,768]{1,0:T(8,128)(2,1)} %get-tuple-element.74) | copy-start | bytes 2949124
  281.4 7.7 %copy-start.1 = (bf16[640,768]{1,0:T(8,128)(2,1)S(1)}, bf16[640,768]{1,0:T(8,128)(2,1)}, u32[]{:S(2)}) copy-start(bf16[640,768]{1,0:T(8,128)(2,1)} %get-tuple-element.62.out_half) | copy-start | bytes 2949124
  289.3 2.3 copy-start
